TPU v7x, 128 devices: a whole 4x4x4 slice. The times are simulated.
128 devices in a mesh: expert: 16 (over y, x), feat: 8 (over z, core).
Axes of the slice: x: 4, y: 4, z: 4, core: 2. Of those that a mesh axis runs over, the one named last changes fastest.
Arguments:
- tokens: bfloat16 [2048, 2304], P('expert'), may hold values from -6 to 6
- expert_ids: int32 [2048, 8], P(('expert', 'feat')), may hold values from 0 to 127, all different within a row; in each aligned block of 16 rows (0 to 15, 16 to 31, ...) at most 2 rows name the same one
- gate_weights: float32 [2048, 8], P(('expert', 'feat')), may hold values from 0.1 to 0.6
- expert_gate: bfloat16 [128, 2304, 1024], P(('expert', 'feat')), may hold values from -0.125 to 0.125
- expert_up: bfloat16 [128, 2304, 1024], P(('expert', 'feat')), may hold values from -0.125 to 0.125
- expert_down: bfloat16 [128, 1024, 2304], P(('expert', 'feat')), may hold values from -0.1875 to 0.1875
- shared_gate: bfloat16 [2304, 1024], P(None, 'feat'), may hold values from -0.125 to 0.125
- shared_up: bfloat16 [2304, 1024], P(None, 'feat'), may hold values from -0.125 to 0.125
- shared_down: bfloat16 [1024, 2304], P('feat'), may hold values from -0.1875 to 0.1875
- encoder: bfloat16 [2304, 65536], P(None, ('expert', 'feat')), may hold values from -0.125 to 0.125
- encoder_bias: float32 [65536], P(('expert', 'feat')), may hold values from -0.6 to 0.2
- decoder: bfloat16 [65536, 2304], P(('expert', 'feat')), may hold values from -0.0234375 to 0.0234375
- decoder_bias: float32 [2304], replicated, may hold values from -3 to 3
Outputs:
- features: bfloat16 [2048, 65536], P(None, ('expert', 'feat'))
- reconstruction: float32 [2048, 2304], P(('expert', 'feat'))
Inputs may be any that keep to these rules, and one draw needn't show every extreme that they name: `expert_ids`: each row names 8 different experts. Within each aligned block of 16 rows (the rows of one device) no expert is named by more than 2 rows, a bound that some block reaches.
All inputs are finite; a program needn't handle non-finite values.
Results may differ from a plain program's by a relative error of at most 0.012.
Values may be sent and summed in bfloat16 or wider, within the bound.
A program may use at most 128 MiB of HBM per device.

v0:
```python
import jax
import jax.numpy as jnp
from jax import lax
from jax.sharding import PartitionSpec as P


def run_experts(received, expert_gate, expert_up, expert_down):
    gate_proj = jnp.einsum(
        "sjcd,jdh->sjch", received, expert_gate, preferred_element_type=jnp.float32
    )
    up_proj = jnp.einsum("sjcd,jdh->sjch", received, expert_up, preferred_element_type=jnp.float32)
    hidden = (jax.nn.silu(gate_proj) * up_proj).astype(jnp.bfloat16)
    return jnp.einsum(
        "sjch,jhd->sjcd", hidden, expert_down, preferred_element_type=jnp.float32
    ).astype(jnp.bfloat16)


def shards(
    tokens,
    expert_ids,
    gate_weights,
    expert_gate,
    expert_up,
    expert_down,
    shared_gate,
    shared_up,
    shared_down,
    encoder,
    encoder_bias,
    decoder,
    decoder_bias,
):
    devices = lax.axis_size(("expert", "feat"))
    own_rows = expert_ids.shape[0]
    top_count = expert_ids.shape[1]
    width = tokens.shape[1]
    local_experts = expert_gate.shape[0]
    experts = local_experts * devices
    cap_slots = max(2, 2 * own_rows * top_count // experts)
    my_tokens = lax.dynamic_slice_in_dim(tokens, lax.axis_index("feat") * own_rows, own_rows, 0)
    flat_ids = expert_ids.reshape(-1)
    onehot = (flat_ids[:, None] == jnp.arange(experts, dtype=jnp.int32)[None, :]).astype(jnp.int32)
    earlier = jnp.cumsum(onehot, axis=0) - onehot
    slot_index = jnp.sum(earlier * onehot, axis=1)
    places = flat_ids * cap_slots + slot_index
    token_owner = jnp.repeat(jnp.arange(own_rows, dtype=jnp.int32), top_count)
    place_hot = (
        places[:, None] == jnp.arange(experts * cap_slots, dtype=jnp.int32)[None, :]
    ).astype(jnp.float32)
    token_hot = (token_owner[:, None] == jnp.arange(own_rows, dtype=jnp.int32)[None, :]).astype(
        jnp.float32
    )
    dispatch_map = jnp.einsum("ps,pt->st", place_hot, token_hot).astype(jnp.bfloat16)
    weighted_hot = token_hot * gate_weights.reshape(-1)[:, None]
    combine_map = jnp.einsum("pt,ps->ts", weighted_hot, place_hot, precision=lax.Precision.HIGHEST)
    outgoing = jnp.dot(dispatch_map, my_tokens, preferred_element_type=jnp.float32).astype(
        jnp.bfloat16
    )
    outgoing = outgoing.reshape(devices, local_experts, cap_slots, width)
    served = run_experts(
        lax.all_to_all(outgoing, ("expert", "feat"), split_axis=0, concat_axis=0, tiled=True),
        expert_gate,
        expert_up,
        expert_down,
    )
    returned = lax.all_to_all(served, ("expert", "feat"), split_axis=0, concat_axis=0, tiled=True)
    returned_rows = returned.reshape(experts * cap_slots, width).astype(jnp.float32)
    routed = jnp.dot(combine_map, returned_rows, precision=lax.Precision.HIGHEST).astype(
        jnp.bfloat16
    )
    shared_gate_proj = jnp.dot(tokens, shared_gate, preferred_element_type=jnp.float32)
    shared_up_proj = jnp.dot(tokens, shared_up, preferred_element_type=jnp.float32)
    shared_hidden = (jax.nn.silu(shared_gate_proj) * shared_up_proj).astype(jnp.bfloat16)
    block_rows = shared_hidden
    shared_out = lax.psum_scatter(
        jnp.dot(block_rows, shared_down, preferred_element_type=jnp.float32),
        "feat",
        scatter_dimension=0,
        tiled=True,
    ).astype(jnp.bfloat16)
    moe_out = (routed.astype(jnp.float32) + shared_out.astype(jnp.float32)).astype(jnp.bfloat16)
    scores = (
        jnp.dot(
            lax.all_gather(moe_out, ("expert", "feat"), axis=0, tiled=True),
            encoder,
            preferred_element_type=jnp.float32,
        )
        + encoder_bias[None, :]
    )
    features = jax.nn.relu(scores).astype(jnp.bfloat16)
    block_rows = features
    reconstruction = (
        lax.psum_scatter(
            jnp.dot(block_rows, decoder, preferred_element_type=jnp.float32),
            ("expert", "feat"),
            scatter_dimension=0,
            tiled=True,
        )
        + decoder_bias[None, :]
    )
    return (features, reconstruction)


def solution(mesh):
    return jax.shard_map(
        shards,
        mesh=mesh,
        in_specs=(
            P("expert", None),
            P(("expert", "feat"), None),
            P(("expert", "feat"), None),
            P(("expert", "feat"), None, None),
            P(("expert", "feat"), None, None),
            P(("expert", "feat"), None, None),
            P(None, "feat"),
            P(None, "feat"),
            P("feat", None),
            P(None, ("expert", "feat")),
            P(("expert", "feat")),
            P(("expert", "feat"), None),
            P(),
        ),
        out_specs=(P(None, ("expert", "feat")), P(("expert", "feat"), None)),
        check_vma=False,
    )
```

profile of v0, /device:TPU:0, one launch (start us, length us, event | category | flops | bytes accessed | tf_op | source)
XLA Modules:
  0.0 415.9 jit_solution(2092600708494928212)
XLA Ops:
  7.2 0.0 copy-start
  7.2 0.9 copy.23
  8.1 0.1 reshape.46
  8.2 0.1 eq.49
  8.3 0.0 copy-start.5
  8.3 0.1 fusion.51
  8.4 0.2 reduce_window_sum.11
  8.6 0.2 select_reduce_fusion
  8.7 0.0 copy-start.6
  8.7 1.7 convolution_convert_fusion
  10.4 1.3 reshape.47
  11.7 0.0 copy-start.1
  11.7 0.0 copy-start.2
  11.7 0.0 copy-done.5
  11.7 0.0 copy-done.6
  11.7 11.6 %all-to-all-start = ((bf16[128,1,2,2304]{3,2,1,0:T(2,128)(2,1)}), bf16[128,1,2,2304]{3,2,1,0:T(2,128)(2,1)}, u32[]{:S(2)}, u32[]{:S(2)}) async-start(bf16[128,1,2,2304]{3,2,1,0:T(2,128)(2,1)} %bitcast), calls=%async_computation | async-start | bytes 2359296 | tf_op jit(solution)/shard_map/all_to_all | solution.py:61
  23.4 0.0 reduce-scatter.3.cloned.1.call-start
  23.4 0.0 copy-done.1
  23.4 0.0 copy-done.2
  23.4 0.9 fusion.63
  24.4 2.9 fusion.33
  27.3 0.0 reduce-scatter.3.cloned.1.call-update
  27.3 16.4 %all-to-all-done = bf16[128,1,2,2304]{3,2,1,0:T(2,128)(2,1)} async-done(((bf16[128,1,2,2304]{3,2,1,0:T(2,128)(2,1)}), bf16[128,1,2,2304]{3,2,1,0:T(2,128)(2,1)}, u32[]{:S(2)}, u32[]{:S(2)}) %all-to-all-start) | async-done | bytes 1179680 | tf_op jit(solution)/shard_map/all_to_all | solution.py:61
  43.7 5.1 %fusion.15 = f32[128,1,2,1024]{3,0,2,1:T(8,128)} fusion(bf16[1,2304,1024]{2,1,0:T(8,128)(2,1)} %param.16, bf16[128,1,2,2304]{3,2,1,0:T(2,128)(2,1)} %all-to-all-done), kind=kOutput, calls=%fused_computation.14 | convolution fusion | flops 1207959552 | bytes 6946816 | tf_op jit(solution)/shard_map/sjcd,jdh->sjch/dot_general | solution.py:8
  48.8 7.2 %fusion.9 = bf16[128,1,2,2304]{3,0,2,1:T(8,128)(2,1)S(1)} fusion(bf16[1,1024,2304]{2,1,0:T(8,128)(2,1)} %param.18, bf16[1,2304,1024]{2,1,0:T(8,128)(2,1)} %param.17, f32[128,1,2,1024]{3,0,2,1:T(8,128)} %fusion.15, bf16[128,1,2,2304]{3,2,1,0:T(2,128)(2,1)} %all-to-all-done), kind=kOutput, calls=%fused_computation.9 | convolution fusion | flops 2418081792 | bytes 12845056 | tf_op jit(solution)/shard_map/sjch,jhd->sjcd/dot_general | solution.py:13
  56.0 0.0 copy-start.4
  56.0 2.2 copy.26
  58.2 4.6 %all-to-all-start.1 = ((bf16[128,1,2,2304]{3,2,1,0:T(2,128)(2,1)}), bf16[128,1,2,2304]{3,2,1,0:T(2,128)(2,1)S(1)}, u32[]{:S(2)}, u32[]{:S(2)}) async-start(bf16[128,1,2,2304]{3,2,1,0:T(2,128)(2,1)} %copy.26), calls=%async_computation.1 | async-start | bytes 2359296 | tf_op jit(solution)/shard_map/all_to_all | solution.py:66
  62.9 0.0 all-gather.2.cloned.1.call-start
  62.9 0.0 copy-done.4
  62.9 0.1 copy.22
  63.0 0.6 mul.40
  63.6 1.0 fusion.41
  64.6 19.0 %all-to-all-done.1 = bf16[128,1,2,2304]{3,2,1,0:T(2,128)(2,1)S(1)} async-done(((bf16[128,1,2,2304]{3,2,1,0:T(2,128)(2,1)}), bf16[128,1,2,2304]{3,2,1,0:T(2,128)(2,1)S(1)}, u32[]{:S(2)}, u32[]{:S(2)}) %all-to-all-start.1) | async-done | bytes 1179680 | tf_op jit(solution)/shard_map/all_to_all | solution.py:66
  83.5 1.3 reshape.53
  84.8 0.0 reduce-scatter.3.cloned.1.call-done
  84.8 2.5 fusion.14
  87.3 0.0 all-gather.2.cloned.1.call-update
  87.3 0.2 reduce-scatter.5.cloned.1.call-start
  87.6 65.9 %all-gather.2.cloned.1.call-done = bf16[2048,2304]{1,0:T(8,128)(2,1)} async-done(((bf16[16,2304]{1,0:T(8,128)(2,1)}), bf16[2048,2304]{1,0:T(8,128)(2,1)}) %all-gather.2.cloned.1.call-update) | async-done | bytes 9437200 | tf_op jit(solution)/shard_map/all_gather | solution.py:84
  153.4 8.3 %maximum_convert_fusion = bf16[2048,512]{1,0:T(8,128)(2,1)S(1)} fusion(bf16[2048,2304]{1,0:T(8,128)(2,1)} %all-gather.2.cloned.1.call-done, bf16[2304,512]{1,0:T(8,128)(2,1)} %param.22, f32[512]{0:T(512)} %param.23), kind=kOutput, calls=%fused_computation.6 | convolution fusion | flops 4834983936 | bytes 13895680 | tf_op jit(solution)/shard_map/dot_general | solution.py:83
  161.7 0.0 copy-start.7
  161.8 1.3 copy-done.7
  163.1 0.0 copy-done
  163.1 9.1 %fusion.64 = f32[2048,2304]{1,0:T(8,128)} fusion(bf16[2048,512]{1,0:T(8,128)(2,1)S(1)} %maximum_convert_fusion, bf16[512,2304]{1,0:T(8,128)(2,1)S(1)} %copy-done), kind=kOutput, calls=%fused_computation.55 | convolution fusion | flops 4831838208 | bytes 23330816 | tf_op jit(solution)/shard_map/dot_general | solution.py:94
  172.2 0.0 copy-start.3
  172.2 0.0 reduce-scatter.5.cloned.1.call-update
  172.2 235.6 %reduce-scatter.5.cloned.1.call-done = f32[16,2304]{1,0:T(8,128)} async-done(((f32[2048,2304]{1,0:T(8,128)}), f32[16,2304]{1,0:T(8,128)}) %reduce-scatter.5.cloned.1.call-update) | async-done | bytes 147472 | tf_op jit(solution)/shard_map/reduce_scatter | solution.py:93
  407.7 0.0 copy-done.3
  407.7 1.6 broadcast_add_fusion
  (2 shorter events, 0.0 us)
Async XLA Ops:
  7.2 155.9 %copy-start = (bf16[512,2304]{1,0:T(8,128)(2,1)S(1)}, bf16[512,2304]{1,0:T(8,128)(2,1)}, u32[]{:S(2)}) copy-start(bf16[512,2304]{1,0:T(8,128)(2,1)} %param.24) | copy-start | bytes 7077892
  8.3 3.4 copy-start.5
  8.7 3.0 copy-start.6
  11.7 11.7 %copy-start.1 = (bf16[128,2304]{1,0:T(8,128)(2,1)S(1)}, bf16[128,2304]{1,0:T(8,128)(2,1)}, u32[]{:S(2)}) copy-start(bf16[128,2304]{1,0:T(8,128)(2,1)} %param.13) | copy-start | bytes 1769476
  11.7 11.7 %copy-start.2 = (bf16[2304,128]{1,0:T(8,128)(2,1)S(1)}, bf16[2304,128]{1,0:T(8,128)(2,1)}, u32[]{:S(2)}) copy-start(bf16[2304,128]{1,0:T(8,128)(2,1)} %param.19) | copy-start | bytes 1769476
  11.7 31.9 %all-to-all-start = ((bf16[128,1,2,2304]{3,2,1,0:T(2,128)(2,1)}), bf16[128,1,2,2304]{3,2,1,0:T(2,128)(2,1)}, u32[]{:S(2)}, u32[]{:S(2)}) async-start(bf16[128,1,2,2304]{3,2,1,0:T(2,128)(2,1)} %bitcast), calls=%async_computation | async-start | bytes 2359296 | tf_op jit(solution)/shard_map/all_to_all | solution.py:61
  23.4 61.5 %reduce-scatter.3.cloned.1.call-start = ((), (), s32[]{:S(2)}) async-start(), calls=%async_computation.4 | async-start | bytes 1327104 | tf_op jit(solution)/shard_map/reduce_scatter | solution.py:75
  56.0 6.9 %copy-start.4 = (f32[16,8]{0,1:T(8,128)S(1)}, f32[16,8]{0,1:T(8,128)}, u32[]{:S(2)}) copy-start(f32[16,8]{0,1:T(8,128)} %param.15) | copy-start | bytes 1540
  58.2 25.3 %all-to-all-start.1 = ((bf16[128,1,2,2304]{3,2,1,0:T(2,128)(2,1)}), bf16[128,1,2,2304]{3,2,1,0:T(2,128)(2,1)S(1)}, u32[]{:S(2)}, u32[]{:S(2)}) async-start(bf16[128,1,2,2304]{3,2,1,0:T(2,128)(2,1)} %copy.26), calls=%async_computation.1 | async-start | bytes 2359296 | tf_op jit(solution)/shard_map/all_to_all | solution.py:66
  62.9 90.5 %all-gather.2.cloned.1.call-start = ((), (), s32[]{:S(2)}) async-start(), calls=%async_computation.5 | async-start | bytes 9510912 | tf_op jit(solution)/shard_map/all_gather | solution.py:84
  87.3 320.4 %reduce-scatter.5.cloned.1.call-start = ((), (), s32[]{:S(2)}) async-start(), calls=%async_computation.6 | async-start | bytes 19021824 | tf_op jit(solution)/shard_map/reduce_scatter | solution.py:93
  161.7 1.3 copy-start.7
  172.2 235.6 %copy-start.3 = (f32[2304]{0:T(1024)S(1)}, f32[2304]{0:T(1024)}, u32[]{:S(2)}) copy-start(f32[2304]{0:T(1024)} %param.25) | copy-start | bytes 27652
Sparse Core Ops, SparseCore 0:
  27.4 33.9 reduce-scatter.2
  87.5 65.9 all-gather.1
  172.3 235.3 reduce-scatter.4
where the time goes:
time: 416 us
  waiting for transfers between devices  337 us (81%)
  matrix products  38.7 us (9%)
  starting transfers between devices  16.6 us (4%)
  between operations  13.9 us (3%)
  local copies, waits for them, and re-layouts  7.89 us (2%)
    reduce_scatter x1, waiting for transfers between devices, shards(): lax.psum_scatter(jnp.dot(block_rows, decoder, preferred_element_type=jnp....  236 us
    all_gather x1, waiting for transfers between devices, shards(): lax.all_gather(moe_out, ('expert', 'feat'), axis=0, tiled=True)  65.9 us
    all_to_all x1, waiting for transfers between devices, shards(): lax.all_to_all(served, ('expert', 'feat'), split_axis=0, concat_axis=0, t...  19 us
    all_to_all x1, waiting for transfers between devices, shards(): lax.all_to_all(outgoing, ('expert', 'feat'), split_axis=0, concat_axis=0,...  16.4 us
    all_to_all x1, starting transfers between devices, shards(): lax.all_to_all(outgoing, ('expert', 'feat'), split_axis=0, concat_axis=0,...  11.6 us
    dot_general x1, matrix products, shards(): jnp.dot(block_rows, decoder, preferred_element_type=jnp.float32)  9.09 us
  transfers between devices with their start and end apart: 5, of which 4 were waited for; matrix products, arithmetic and copies ran while one was open for 5% of the time, Pallas kernels for 0%

commit v1 on v0

--- a/solution.py
+++ b/solution.py
@@ -1,7 +1,354 @@
+import functools
+
 import jax
 import jax.numpy as jnp
 from jax import lax
+from jax.experimental import pallas as pl
+from jax.experimental.pallas import tpu as pltpu
 from jax.sharding import PartitionSpec as P
+
+MESH = pl.DeviceIdType.MESH
+SIDE = 4
+ORDERS = ((1, 0, 2), (0, 2, 1), (2, 1, 0))
+PARTS = len(ORDERS)
+ALL = slice(None)
+
+
+def sae_kernel(
+    rows_ref, enc_hbm, bias_ref, dec_hbm, dec_bias_ref, feat_hbm, rec_ref,
+    gathered, feats, enc, dec, out_half, in_half, total, land0, land1, land2,
+    ag_send, ag_recv, cross_send, cross_recv, half_send, half_recv, rs_send, rs_recv, local_sem, feat_sem,
+):
+    e, f = lax.axis_index("expert"), lax.axis_index("feat")
+    core = lax.rem(f, 2)
+    other = 1 - core
+    pos = (e // SIDE, lax.rem(e, SIDE), f // 2)
+    lands = (land0, land1, land2)
+    width = gathered.shape[-1]
+    hid = width // 2
+
+    def at(axis, delta):
+        return lax.rem(pos[axis] + delta + SIDE, SIDE)
+
+    def device(axis, delta):
+        there = list(pos)
+        there[axis] = at(axis, delta)
+        return (there[0] * SIDE + there[1], there[2] * 2 + core)
+
+    partner = (e, f + 1 - 2 * core)
+
+    def remote(src, dst, send, recv, where):
+        return pltpu.make_async_remote_copy(
+            src_ref=src, dst_ref=dst, send_sem=send, recv_sem=recv, device_id=where, device_id_type=MESH
+        )
+
+    locals_ = [
+        pltpu.make_async_copy(enc_hbm, enc, local_sem.at[0]),
+        pltpu.make_async_copy(dec_hbm, dec, local_sem.at[1]),
+    ]
+    for part in range(PARTS):
+        locals_.append(
+            pltpu.make_async_copy(
+                rows_ref.at[:, pl.ds(part * width, width)],
+                gathered.at[part, core, pos[0], pos[1], pos[2]],
+                local_sem.at[2 + part],
+            )
+        )
+    for copy in locals_:
+        copy.start()
+
+    barrier = pltpu.get_barrier_semaphore()
+    neighbours = [device(axis, delta) for axis in range(3) for delta in (1, -1)] + [partner]
+    for there in neighbours:
+        pl.semaphore_signal(barrier, inc=1, device_id=there, device_id_type=MESH)
+    pl.semaphore_wait(barrier, len(neighbours))
+
+    def ag_cells(part, stage, k, half, which):
+        order = ORDERS[part]
+        idx = list(pos)
+        for axis in order[:stage]:
+            idx[axis] = ALL
+        idx[order[stage]] = k
+        cols = ALL
+        if half is not None:
+            if stage:
+                idx[order[0]] = pl.ds(2 * half, 2)
+            else:
+                cols = pl.ds(hid * half, hid)
+        return gathered.at[(part, which, *idx, ALL, cols)]
+
+    ag = {}
+
+    def ag_start(part, stage, j, src, k, half, delta):
+        copy = remote(
+            src,
+            ag_cells(part, stage, k, half, core),
+            ag_send.at[stage, part, j],
+            ag_recv.at[stage, part, j],
+            device(ORDERS[part][stage], delta),
+        )
+        copy.start()
+        ag[part, stage, j] = copy
+
+    AG_FROM = ((-1, 0), (1, 1), (-1, 1), (1, 0), (-2, 0), (2, 1))
+
+    def ag_landed(part, stage, j):
+        delta, half = AG_FROM[j]
+        cells = ag_cells(part, stage, at(ORDERS[part][stage], delta), half, core)
+        remote(
+            cells, cells, ag_send.at[stage, part, j], ag_recv.at[stage, part, j],
+            device(ORDERS[part][stage], 1),
+        ).wait_recv()
+        return cells
+
+    cross = []
+
+    def cross_start(part, j, cells):
+        copy = remote(cells, cells, cross_send.at[part, j], cross_recv.at[part, j], partner)
+        copy.start()
+        cross.append(copy)
+
+    for stage in range(3):
+        for part in range(PARTS):
+            axis = ORDERS[part][stage]
+            here = pos[axis]
+            for j, (delta, half) in enumerate(((1, 0), (-1, 1), (1, 1), (-1, 0))):
+                if stage == 0:
+                    src = rows_ref.at[:, pl.ds(part * width + hid * half, hid)]
+                else:
+                    src = ag_cells(part, stage, here, half, core)
+                ag_start(part, stage, j, src, here, half, delta)
+            if stage == 2:
+                cross_start(part, 6, ag_cells(part, stage, here, None, core))
+        for part in range(PARTS):
+            axis = ORDERS[part][stage]
+            for j, delta in ((0, 1), (1, -1)):
+                cells = ag_landed(part, stage, j)
+                ag_start(part, stage, 4 + j, cells, at(axis, -delta), AG_FROM[j][1], delta)
+                if stage == 2:
+                    cross_start(part, j, cells)
+        for j in (2, 3, 4, 5):
+            for part in range(PARTS):
+                cells = ag_landed(part, stage, j)
+                if stage == 2:
+                    cross_start(part, j, cells)
+        if stage == 0:
+            for copy in locals_:
+                copy.wait()
+    for part in range(PARTS):
+        axis = ORDERS[part][2]
+        for j in range(7):
+            delta, half = AG_FROM[j] if j < 6 else (0, None)
+            cells = ag_cells(part, 2, at(axis, delta), half, other)
+            remote(cells, cells, cross_send.at[part, j], cross_recv.at[part, j], partner).wait_recv()
+
+    features = enc.shape[1]
+
+    def encode(step, carry):
+        which, y = step // 2, 2 * lax.rem(step, 2)
+        rows = 2 * SIDE * SIDE * 16
+        scores = bias_ref[...].astype(jnp.float32)
+        for part in range(PARTS):
+            block = gathered[part, which, pl.ds(y, 2)].reshape(rows, width)
+            scores = scores + jnp.dot(
+                block, enc[part * width : (part + 1) * width, :], preferred_element_type=jnp.float32
+            )
+        feats[which, pl.ds(y, 2)] = (
+            jnp.maximum(scores, 0.0).astype(jnp.bfloat16).reshape(2, SIDE, SIDE, 16, features)
+        )
+        return carry
+
+    lax.fori_loop(0, 4, encode, 0)
+    feat_copies = []
+    for which in range(2):
+        copy = pltpu.make_async_copy(feats.at[which], feat_hbm.at[:, :, :, which], feat_sem.at[which])
+        copy.start()
+        feat_copies.append(copy)
+
+    def cells_of(part, stage, k, half):
+        order = ORDERS[part]
+        left = order[: 2 - stage]
+        idx = list(pos)
+        for axis in left:
+            idx[axis] = ALL
+        idx[order[2 - stage]] = k
+        cols = ALL
+        if half is not None:
+            if left:
+                idx[order[0]] = pl.ds(2 * half, 2)
+            else:
+                cols = pl.ds(hid * half, hid)
+        return (*idx, ALL, cols)
+
+    def land_of(part, stage, kind, half):
+        order = ORDERS[part]
+        left = sorted(order[: 2 - stage])
+        idx = [ALL for _ in left]
+        cols = ALL
+        if half is not None:
+            if left:
+                idx[left.index(order[0])] = pl.ds(2 * half, 2)
+            else:
+                cols = pl.ds(hid * half, hid)
+        return (part, kind, *idx, ALL, cols)
+
+    def product(part, delta, which):
+        idx = cells_of(part, 0, at(ORDERS[part][2], delta), None)
+        block = feats[(which, *idx)].reshape(SIDE * SIDE * 16, features)
+        return jnp.dot(
+            block, dec[:, part * width : (part + 1) * width], preferred_element_type=jnp.float32
+        ).reshape(SIDE, SIDE, 16, width)
+
+    halves = []
+
+    def half_copy(part, delta):
+        idx = cells_of(part, 0, at(ORDERS[part][2], delta), None)
+        return remote(
+            out_half.at[(part, *idx)],
+            in_half.at[(part, *idx)],
+            half_send.at[part, delta + 1],
+            half_recv.at[part, delta + 1],
+            partner,
+        )
+
+    def give(part, delta):
+        idx = cells_of(part, 0, at(ORDERS[part][2], delta), None)
+        out_half[(part, *idx)] = product(part, delta, other).astype(jnp.bfloat16)
+        copy = half_copy(part, delta)
+        copy.start()
+        halves.append(copy)
+
+    def keep(part, delta):
+        idx = cells_of(part, 0, at(ORDERS[part][2], delta), None)
+        mine = product(part, delta, core)
+        half_copy(part, delta).wait_recv()
+        total[(part, *idx)] = (mine + in_half[(part, *idx)].astype(jnp.float32)).astype(jnp.bfloat16)
+
+    MINUS, PLUS, FAR = 0, 1, 2
+    RS_COPIES = (
+        (2, 0, 1, FAR), (2, 1, -1, FAR), (1, 1, 1, MINUS), (-1, 0, -1, PLUS), (1, 0, 1, MINUS), (-1, 1, -1, PLUS),
+    )
+    rs = []
+
+    def rs_copy(part, stage, j):
+        delta, half, way, kind = RS_COPIES[j]
+        axis = ORDERS[part][2 - stage]
+        return remote(
+            total.at[(part, *cells_of(part, stage, at(axis, delta), half))],
+            lands[stage].at[land_of(part, stage, kind, half)],
+            rs_send.at[stage, part, j],
+            rs_recv.at[stage, part, j],
+            device(axis, way),
+        )
+
+    def rs_start(part, stage, j):
+        copy = rs_copy(part, stage, j)
+        copy.start()
+        rs.append(copy)
+
+    def pass_on(part, stage):
+        for j in (0, 1):
+            rs_copy(part, stage, j).wait_recv()
+            _, half, way, _ = RS_COPIES[j]
+            idx = (part, *cells_of(part, stage, at(ORDERS[part][2 - stage], way), half))
+            far = lands[stage][land_of(part, stage, FAR, half)]
+            total[idx] = (total[idx].astype(jnp.float32) + far.astype(jnp.float32)).astype(jnp.bfloat16)
+            rs_start(part, stage, 4 + j)
+
+    def own_sum(part, stage):
+        for j in (2, 3, 4, 5):
+            rs_copy(part, stage, j).wait_recv()
+        idx = (part, *cells_of(part, stage, pos[ORDERS[part][2 - stage]], None))
+        value = total[idx].astype(jnp.float32)
+        for kind in (MINUS, PLUS):
+            value = value + lands[stage][land_of(part, stage, kind, None)].astype(jnp.float32)
+        return idx, value
+
+    for part in range(PARTS):
+        give(part, 2)
+    for part in range(PARTS):
+        keep(part, 2)
+        rs_start(part, 0, 0)
+        rs_start(part, 0, 1)
+    for part in range(PARTS):
+        give(part, 1)
+        give(part, -1)
+    for part in range(PARTS):
+        keep(part, 1)
+        rs_start(part, 0, 2)
+        keep(part, -1)
+        rs_start(part, 0, 3)
+    for part in range(PARTS):
+        give(part, 0)
+    for part in range(PARTS):
+        pass_on(part, 0)
+    for part in range(PARTS):
+        keep(part, 0)
+    for stage in range(3):
+        if stage:
+            for part in range(PARTS):
+                pass_on(part, stage)
+        for part in range(PARTS):
+            idx, value = own_sum(part, stage)
+            if stage < 2:
+                total[idx] = value.astype(jnp.bfloat16)
+                for j in range(4):
+                    rs_start(part, stage + 1, j)
+            else:
+                cols = slice(part * width, (part + 1) * width)
+                rec_ref[:, cols] = value + dec_bias_ref[:, cols]
+
+    for copy in list(ag.values()) + cross + halves + rs:
+        copy.wait_send()
+    for copy in feat_copies:
+        copy.wait()
+
+
+def sae(rows, encoder, encoder_bias, decoder, decoder_bias):
+    own_rows, model = rows.shape
+    features = encoder.shape[1]
+    width = model // PARTS
+    cube = (SIDE, SIDE, SIDE)
+    bf16 = jnp.bfloat16
+    vmem = pl.BlockSpec(memory_space=pltpu.VMEM)
+    hbm = pl.BlockSpec(memory_space=pl.ANY)
+    dma = pltpu.SemaphoreType.DMA
+    out, rec = pl.pallas_call(
+        sae_kernel,
+        name="sae",
+        out_shape=(
+            jax.ShapeDtypeStruct((*cube, 2, own_rows, features), bf16),
+            jax.ShapeDtypeStruct((own_rows, model), jnp.float32),
+        ),
+        in_specs=[vmem, hbm, vmem, hbm, vmem],
+        out_specs=(hbm, vmem),
+        scratch_shapes=[
+            pltpu.VMEM((PARTS, 2, *cube, own_rows, width), bf16),
+            pltpu.VMEM((2, *cube, own_rows, features), bf16),
+            pltpu.VMEM((model, features), bf16),
+            pltpu.VMEM((features, model), bf16),
+            pltpu.VMEM((PARTS, *cube, own_rows, width), bf16),
+            pltpu.VMEM((PARTS, *cube, own_rows, width), bf16),
+            pltpu.VMEM((PARTS, *cube, own_rows, width), bf16),
+            pltpu.VMEM((PARTS, 3, SIDE, SIDE, own_rows, width), bf16),
+            pltpu.VMEM((PARTS, 3, SIDE, own_rows, width), bf16),
+            pltpu.VMEM((PARTS, 3, own_rows, width), bf16),
+            dma((3, PARTS, 6)),
+            dma((3, PARTS, 6)),
+            dma((PARTS, 7)),
+            dma((PARTS, 7)),
+            dma((PARTS, 4)),
+            dma((PARTS, 4)),
+            dma((3, PARTS, 6)),
+            dma((3, PARTS, 6)),
+            dma((2 + PARTS,)),
+            dma((2,)),
+        ],
+        compiler_params=pltpu.CompilerParams(
+            collective_id=0, has_side_effects=True, vmem_limit_bytes=60 * 1024 * 1024
+        ),
+    )(rows, encoder, encoder_bias[None, :], decoder, decoder_bias[None, :])
+    return out.reshape(-1, features), rec
 
 
 def run_experts(received, expert_gate, expert_up, expert_down):
@@ -79,26 +426,7 @@
         tiled=True,
     ).astype(jnp.bfloat16)
     moe_out = (routed.astype(jnp.float32) + shared_out.astype(jnp.float32)).astype(jnp.bfloat16)
-    scores = (
-        jnp.dot(
-            lax.all_gather(moe_out, ("expert", "feat"), axis=0, tiled=True),
-            encoder,
-            preferred_element_type=jnp.float32,
-        )
-        + encoder_bias[None, :]
-    )
-    features = jax.nn.relu(scores).astype(jnp.bfloat16)
-    block_rows = features
-    reconstruction = (
-        lax.psum_scatter(
-            jnp.dot(block_rows, decoder, preferred_element_type=jnp.float32),
-            ("expert", "feat"),
-            scatter_dimension=0,
-            tiled=True,
-        )
-        + decoder_bias[None, :]
-    )
-    return (features, reconstruction)
+    return sae(moe_out, encoder, encoder_bias, decoder, decoder_bias)
 
 
 def solution(mesh):

time: 416 us -> 169 us (0.41)
  waiting for transfers between devices: 337 us -> 36.5 us
  Pallas kernels: 0 us -> 73.2 us
  matrix products: 38.7 us -> 18.2 us
    reduce_scatter x1 -> x0, waiting for transfers between devices: 236 us -> none  [shards(): lax.psum_scatter(jnp.dot(block_rows, decoder, preferred_element_type=jnp....]
    pallas_call x0 -> x1, Pallas kernels: none -> 73.2 us  [sae(): pl.pallas_call(sae_kernel, name='sae', out_shape=(jax.ShapeDtypeStruct((*...]
    all_gather x1 -> x0, waiting for transfers between devices: 65.9 us -> none  [shards(): lax.all_gather(moe_out, ('expert', 'feat'), axis=0, tiled=True)]
    dot_general x2 -> x0, matrix products: 17.4 us -> none  [the longest x1 9.09 us: shards(): jnp.dot(block_rows, decoder, preferred_element_type=jnp.float32)]
  transfers between devices with their start and end apart: 5 -> 3, of which waited for: 4 -> 2; matrix products, arithmetic and copies ran while one was open for 5% -> 11% of each run, Pallas kernels for 0% -> 0%
where the time goes in v1:
time: 169 us; the launch traced here: 168 us
  Pallas kernels  73.2 us (43%)
  waiting for transfers between devices  36.5 us (22%)
  matrix products  18.2 us (11%)
  starting transfers between devices  16 us (9%)
  between operations  14.2 us (8%)
  local copies, waits for them, and re-layouts  9.72 us (6%)
    pallas_call x1, Pallas kernels, sae(): pl.pallas_call(sae_kernel, name='sae', out_shape=(jax.ShapeDtypeStruct((*...  73.2 us
    all_to_all x1, waiting for transfers between devices, shards(): lax.all_to_all(served, ('expert', 'feat'), split_axis=0, concat_axis=0, t...  19.6 us
    all_to_all x1, waiting for transfers between devices, shards(): lax.all_to_all(outgoing, ('expert', 'feat'), split_axis=0, concat_axis=0,...  16.9 us
    all_to_all x1, starting transfers between devices, shards(): lax.all_to_all(outgoing, ('expert', 'feat'), split_axis=0, concat_axis=0,...  11.2 us
    dot_general x1, matrix products, run_experts(): jnp.einsum('sjch,jhd->sjcd', hidden, expert_down, preferred_element_type=...  6.87 us
    unnamed x18, local copies, waits for them, and re-layouts  4.87 us
    all_to_all x1, starting transfers between devices, shards(): lax.all_to_all(served, ('expert', 'feat'), split_axis=0, concat_axis=0, t...  4.76 us
    dot_general x1, matrix products, run_experts(): jnp.einsum('sjcd,jdh->sjch', received, expert_gate, preferred_element_typ...  4.74 us
  transfers between devices with their start and end apart: 3, of which 2 were waited for; matrix products, arithmetic and copies ran while one was open for 11% of the time, Pallas kernels for 0%

profile of v1, /device:TPU:0, one launch (start us, length us, event | category | flops | bytes accessed | tf_op | source)
XLA Modules:
  0.0 168.3 jit_solution(2872125148505942264)
XLA Ops:
  7.2 0.0 copy-start
  7.2 0.8 copy.23
  8.0 0.1 reshape.47
  8.1 0.1 eq.49
  8.2 0.1 fusion.51
  8.3 0.2 reduce_window_sum.11
  8.5 0.2 select_reduce_fusion
  8.6 0.0 copy-done
  8.7 0.8 convolution_convert_fusion
  9.4 1.3 reshape.48
  10.7 0.0 copy-start.1
  10.7 11.2 %all-to-all-start = ((bf16[128,1,2,2304]{3,2,1,0:T(2,128)(2,1)}), bf16[128,1,2,2304]{3,2,1,0:T(2,128)(2,1)S(1)}, u32[]{:S(2)}, u32[]{:S(2)}) async-start(bf16[128,1,2,2304]{3,2,1,0:T(2,128)(2,1)} %bitcast), calls=%async_computation | async-start | bytes 2359296 | tf_op jit(solution)/shard_map/all_to_all | solution.py:408
  21.9 0.0 copy-start.2
  21.9 0.0 copy-start.3
  21.9 0.0 reduce-scatter.2.cloned.1.call-start
  22.0 0.0 copy-done.1
  22.0 1.0 fusion.63
  22.9 0.0 copy-done.2
  23.0 0.2 copy-done.3
  23.1 2.5 %fusion.33 = f32[128,2304]{1,0:T(8,128)} fusion(bf16[128,2304]{1,0:T(8,128)(2,1)S(1)} %copy-done.2, bf16[128,2304]{1,0:T(8,128)(2,1)S(1)} %copy-done, bf16[2304,128]{1,0:T(8,128)(2,1)S(1)} %copy-done.3, f32[128,128]{1,0:T(8,128)} %fusion.63), kind=kOutput, calls=%fused_computation.22 | convolution fusion | flops 151093248 | bytes 3014656 | tf_op jit(solution)/shard_map/dot_general | solution.py:423
  25.6 0.0 reduce-scatter.2.cloned.1.call-update
  25.6 16.9 %all-to-all-done = bf16[128,1,2,2304]{3,2,1,0:T(2,128)(2,1)S(1)} async-done(((bf16[128,1,2,2304]{3,2,1,0:T(2,128)(2,1)}), bf16[128,1,2,2304]{3,2,1,0:T(2,128)(2,1)S(1)}, u32[]{:S(2)}, u32[]{:S(2)}) %all-to-all-start) | async-done | bytes 1179680 | tf_op jit(solution)/shard_map/all_to_all | solution.py:408
  42.6 4.7 %fusion.15 = f32[128,1,2,1024]{3,0,2,1:T(8,128)} fusion(bf16[1,2304,1024]{2,1,0:T(8,128)(2,1)} %param.16, bf16[128,1,2,2304]{3,2,1,0:T(2,128)(2,1)S(1)} %all-to-all-done), kind=kOutput, calls=%fused_computation.13 | convolution fusion | flops 1207959552 | bytes 6946816 | tf_op jit(solution)/shard_map/sjcd,jdh->sjch/dot_general | solution.py:355
  47.3 6.9 %fusion.9 = bf16[128,1,2,2304]{3,0,2,1:T(8,128)(2,1)S(1)} fusion(bf16[1,1024,2304]{2,1,0:T(8,128)(2,1)} %param.18, bf16[1,2304,1024]{2,1,0:T(8,128)(2,1)} %param.17, f32[128,1,2,1024]{3,0,2,1:T(8,128)} %fusion.15, bf16[128,1,2,2304]{3,2,1,0:T(2,128)(2,1)S(1)} %all-to-all-done), kind=kOutput, calls=%fused_computation.8 | convolution fusion | flops 2418081792 | bytes 12845056 | tf_op jit(solution)/shard_map/sjch,jhd->sjcd/dot_general | solution.py:360
  54.2 2.2 %copy.26 = bf16[128,1,2,2304]{3,2,1,0:T(2,128)(2,1)} copy(bf16[128,1,2,2304]{3,0,2,1:T(8,128)(2,1)S(1)} %fusion.9) | data formatting | bytes 2359296 | tf_op jit(solution)/shard_map/convert_element_type | solution.py:362
  56.4 0.0 copy-start.6
  56.4 0.0 copy-start.5
  56.4 4.8 %all-to-all-start.1 = ((bf16[128,1,2,2304]{3,2,1,0:T(2,128)(2,1)}), bf16[128,1,2,2304]{3,2,1,0:T(2,128)(2,1)S(1)}, u32[]{:S(2)}, u32[]{:S(2)}) async-start(bf16[128,1,2,2304]{3,2,1,0:T(2,128)(2,1)} %copy.26), calls=%async_computation.1 | async-start | bytes 2359296 | tf_op jit(solution)/shard_map/all_to_all | solution.py:413
  61.2 0.0 copy-done.6
  61.2 0.1 copy.22
  61.3 0.1 mul.40
  61.3 0.0 copy-done.5
  61.4 0.6 broadcast_in_dim.17.dec_bias_ref
  62.0 0.3 fusion.41
  62.2 19.6 %all-to-all-done.1 = bf16[128,1,2,2304]{3,2,1,0:T(2,128)(2,1)S(1)} async-done(((bf16[128,1,2,2304]{3,2,1,0:T(2,128)(2,1)}), bf16[128,1,2,2304]{3,2,1,0:T(2,128)(2,1)S(1)}, u32[]{:S(2)}, u32[]{:S(2)}) %all-to-all-start.1) | async-done | bytes 1179680 | tf_op jit(solution)/shard_map/all_to_all | solution.py:413
  81.8 0.5 reshape.54
  82.3 0.0 reduce-scatter.2.cloned.1.call-done
  82.3 2.1 %fusion.14.rows_ref = bf16[16,2304]{1,0:T(8,128)(2,1)} fusion(f32[16,256]{1,0:T(8,128)S(1)} %fusion.41, bf16[256,2304]{1,0:T(8,128)(2,1)S(1)} %reshape.54, f32[16,2304]{1,0:T(8,128)} %reduce-scatter.2.cloned.1.call-done), kind=kOutput, calls=%fused_computation.12 | convolution fusion | flops 113467392 | bytes 1417216 | tf_op jit(solution)/shard_map/dot_general | solution.py:415
  84.5 73.2 %sae.1 = (bf16[4,4,4,2,16,512]{5,4,3,2,1,0:T(8,128)(2,1)}, f32[16,2304]{1,0:T(8,128)}) custom-call(bf16[16,2304]{1,0:T(8,128)(2,1)} %fusion.14.rows_ref, bf16[2304,512]{1,0:T(8,128)(2,1)} %enc_hbm.1, f32[1,512]{1,0:T(1,128)} %bitcast.76, bf16[512,2304]{1,0:T(8,128)(2,1)} %dec_hbm.1, f32[1,2304]{1,0:T(1,128)} %broadcast_in_dim.17.dec_bias_ref), custom_call_target="tpu_custom_call" | custom-call | tf_op jit(solution)/shard_map/sae/pallas_call | solution.py:316
  157.7 0.0 copy-start.4
  157.7 3.1 %copy.39 = bf16[2048,512]{1,0:T(8,128)(2,1)} copy(bf16[2048,512]{1,0:T(8,128)(2,1)} %bitcast.75) | data formatting | bytes 4194304
  160.8 0.0 copy-done.4
  160.8 0.7 copy.40
  (2 shorter events, 0.0 us)
Async XLA Ops:
  7.2 1.5 copy-start
  10.7 11.3 %copy-start.1 = (bf16[2304,128]{1,0:T(8,128)(2,1)S(1)}, bf16[2304,128]{1,0:T(8,128)(2,1)}, u32[]{:S(2)}) copy-start(bf16[2304,128]{1,0:T(8,128)(2,1)} %param.19) | copy-start | bytes 1769476
  10.7 31.8 %all-to-all-start = ((bf16[128,1,2,2304]{3,2,1,0:T(2,128)(2,1)}), bf16[128,1,2,2304]{3,2,1,0:T(2,128)(2,1)S(1)}, u32[]{:S(2)}, u32[]{:S(2)}) async-start(bf16[128,1,2,2304]{3,2,1,0:T(2,128)(2,1)} %bitcast), calls=%async_computation | async-start | bytes 2359296 | tf_op jit(solution)/shard_map/all_to_all | solution.py:408
  21.9 1.1 copy-start.2
  21.9 1.2 copy-start.3
  21.9 60.4 %reduce-scatter.2.cloned.1.call-start = ((), (), s32[]{:S(2)}) async-start(), calls=%async_computation.3 | async-start | bytes 1327104 | tf_op jit(solution)/shard_map/reduce_scatter | solution.py:422
  56.4 4.8 %copy-start.6 = (f32[16,8]{0,1:T(8,128)S(1)}, f32[16,8]{0,1:T(8,128)}, u32[]{:S(2)}) copy-start(f32[16,8]{0,1:T(8,128)} %param.15) | copy-start | bytes 1540
  56.4 4.9 %copy-start.5 = (f32[2304]{0:T(1024)S(1)}, f32[2304]{0:T(1024)}, u32[]{:S(2)}) copy-start(f32[2304]{0:T(1024)} %param.25) | copy-start | bytes 27652
  56.4 25.4 %all-to-all-start.1 = ((bf16[128,1,2,2304]{3,2,1,0:T(2,128)(2,1)}), bf16[128,1,2,2304]{3,2,1,0:T(2,128)(2,1)S(1)}, u32[]{:S(2)}, u32[]{:S(2)}) async-start(bf16[128,1,2,2304]{3,2,1,0:T(2,128)(2,1)} %copy.26), calls=%async_computation.1 | async-start | bytes 2359296 | tf_op jit(solution)/shard_map/all_to_all | solution.py:413
  157.7 3.1 %copy-start.4 = (f32[16,2304]{1,0:T(8,128)S(1)}, f32[16,2304]{1,0:T(8,128)}, u32[]{:S(2)}) copy-start(f32[16,2304]{1,0:T(8,128)} %get-tuple-element.9) | copy-start | bytes 442372
Sparse Core Ops, SparseCore 0:
  25.8 34.6 reduce-scatter.1

commit v2 on v0

v2 whole, which is shorter than its diff:
```python
import jax
import jax.numpy as jnp
from jax import lax
from jax.experimental import pallas as pl
from jax.experimental.pallas import tpu as pltpu
from jax.sharding import PartitionSpec as P

MESH = pl.DeviceIdType.MESH
SIDE = 4
ORDERS = ((1, 0, 2), (0, 2, 1), (2, 1, 0))
PARTS = len(ORDERS)
ALL = slice(None)
BF16 = jnp.bfloat16
F32 = jnp.float32
OUTWARD = (0, 1, -1, 2)
INWARD = (2, 1, -1, 0)
FAR_WAY = {0: 1, 2: 1, 1: -1, -1: -1}
FAR, MINUS, PLUS = 0, 1, 2
OTHERS = (1, -1, 2)
TOP = 8
COPIES = 18


class Torus:
    def __init__(self):
        self.e, self.f = lax.axis_index("expert"), lax.axis_index("feat")
        self.core = lax.rem(self.f, 2)
        self.other = 1 - self.core
        self.pos = (self.e // SIDE, lax.rem(self.e, SIDE), self.f // 2)
        self.partner = (self.e, self.f + 1 - 2 * self.core)

    def at(self, axis, delta):
        return lax.rem(self.pos[axis] + delta + SIDE, SIDE) if delta else self.pos[axis]

    def device(self, axis, delta):
        there = list(self.pos)
        there[axis] = self.at(axis, delta)
        return (there[0] * SIDE + there[1], there[2] * 2 + self.core)

    def index(self, part, offsets):
        idx = [None] * 3
        for axis, delta in zip(ORDERS[part], offsets):
            idx[axis] = ALL if delta is None else self.at(axis, delta)
        return tuple(idx)

    def meet(self, peers):
        barrier = pltpu.get_barrier_semaphore()
        for there in peers:
            pl.semaphore_signal(barrier, inc=1, device_id=there, device_id_type=MESH)
        pl.semaphore_wait(barrier, len(peers))


def remote(src, dst, send, recv, where):
    return pltpu.make_async_remote_copy(
        src_ref=src, dst_ref=dst, send_sem=send, recv_sem=recv, device_id=where, device_id_type=MESH
    )


class Gather:
    def __init__(self, torus, own, buf, send, recv):
        self.torus, self.own, self.buf, self.send, self.recv = torus, own, buf, send, recv
        self.specs = [(0, d, (0, 0, 0), (-d, 0, 0)) for d in OTHERS]
        self.specs += [(1, d, (None, 0, 0), (None, -d, 0)) for d in OTHERS]
        for d in OUTWARD:
            way = FAR_WAY[d]
            self.specs += [
                (2, 1, (None, d, 0), (None, d, -1)),
                (2, -1, (None, d, 0), (None, d, 1)),
                (2, way, (None, d, -way), (None, d, 2)),
            ]
        self.started = []

    def cells(self, part, offsets):
        return self.buf.at[(part, *self.torus.index(part, offsets))]

    def copy(self, part, k, landing):
        slot, delta, source, target = self.specs[k]
        dst = self.cells(part, target if landing else source)
        src = self.own(part) if source == (0, 0, 0) and not landing else dst
        return remote(
            src, dst, self.send.at[part, k], self.recv.at[part, k], self.torus.device(ORDERS[part][slot], delta)
        )

    def start(self, part, *ks):
        for k in ks:
            copy = self.copy(part, k, False)
            copy.start()
            self.started.append(copy)

    def wait(self, part, *ks):
        for k in ks:
            self.copy(part, k, True).wait_recv()

    def run(self, own_ready):
        parts = range(PARTS)
        plane = {d: 6 + 3 * i for i, d in enumerate(OUTWARD)}
        for p in parts:
            self.start(p, 0, 1, 2)
        own_ready()
        for p in parts:
            self.wait(p, 0, 1, 2)
            self.start(p, 3, 4, 5)
        for p in parts:
            self.start(p, plane[0], plane[0] + 1)
        for i, d in enumerate(OTHERS):
            for p in parts:
                self.wait(p, 3 + i)
                self.start(p, plane[-d if d != 2 else 2], plane[-d if d != 2 else 2] + 1)
            if i == 1:
                for p in parts:
                    self.wait(p, plane[0], plane[0] + 1)
                    self.start(p, plane[0] + 2)
        for d in (-1, 1, 2):
            for p in parts:
                self.wait(p, plane[d], plane[d] + 1)
                self.start(p, plane[d] + 2)
        for p in parts:
            for d in OUTWARD:
                self.wait(p, plane[d] + 2)

    def drain(self):
        for copy in self.started:
            copy.wait_send()


class Scatter:
    def __init__(self, torus, total, planes, lines, blocks, send, recv):
        self.torus, self.total, self.send, self.recv = torus, total, send, recv
        self.specs = []
        for i, d in enumerate(INWARD):
            for way, last, kind in ((FAR_WAY[d], 2, FAR), (1, 1, MINUS), (-1, -1, PLUS)):
                self.specs.append((2, way, (None, d, last), planes, (kind, i)))
        self.specs += [(1, d, (None, d, 0), lines, (i,)) for i, d in enumerate(INWARD[:3])]
        self.specs += [(0, d, (d, 0, 0), blocks, (i,)) for i, d in enumerate(INWARD[:3])]
        self.started = []

    def cells(self, part, offsets):
        return (part, *self.torus.index(part, offsets))

    def copy(self, part, k):
        slot, delta, source, lands, place = self.specs[k]
        return remote(
            self.total.at[self.cells(part, source)],
            lands.at[(part, *place)],
            self.send.at[part, k],
            self.recv.at[part, k],
            self.torus.device(ORDERS[part][slot], delta),
        )

    def start(self, part, *ks):
        for k in ks:
            copy = self.copy(part, k)
            copy.start()
            self.started.append(copy)

    def landed(self, part, k):
        self.copy(part, k).wait_recv()
        _, _, _, lands, place = self.specs[k]
        return lands[(part, *place)].astype(F32)

    def add(self, part, offsets, ks):
        idx = self.cells(part, offsets)
        value = self.total[idx].astype(F32)
        for k in ks:
            value = value + self.landed(part, k)
        return idx, value

    def run(self, produce, finish):
        parts = range(PARTS)
        plane = {d: 3 * i for i, d in enumerate(INWARD)}

        def raw(p, way):
            for d in INWARD:
                if FAR_WAY[d] != way:
                    self.start(p, plane[d] + (1 if way == 1 else 2))

        for p in parts:
            produce(p, 2)
            self.start(p, *(plane[d] for d in INWARD))
        for p in parts:
            produce(p, 1)
            raw(p, 1)
            produce(p, -1)
            raw(p, -1)
        for p in parts:
            produce(p, 0)
        for d in INWARD:
            way = FAR_WAY[d]
            for p in parts:
                idx, value = self.add(p, (None, d, way), (plane[d],))
                self.total[idx] = value.astype(BF16)
                self.start(p, plane[d] + (1 if way == 1 else 2))
        for i, d in enumerate(INWARD):
            for p in parts:
                idx, value = self.add(p, (None, d, 0), (plane[d] + 1, plane[d] + 2))
                self.total[idx] = value.astype(BF16)
                if d:
                    self.start(p, 12 + i)
        for p in parts:
            idx, value = self.add(p, (None, 0, 0), (12, 13, 14))
            self.total[idx] = value.astype(BF16)
            self.start(p, 15, 16, 17)
        for p in parts:
            _, value = self.add(p, (0, 0, 0), (15, 16, 17))
            finish(p, value)

    def drain(self):
        for copy in self.started:
            copy.wait_send()


def torus_scratch(rows, width):
    cube = (SIDE, SIDE, SIDE)
    dma = pltpu.SemaphoreType.DMA((PARTS, COPIES))
    return [
        pltpu.VMEM((PARTS, *cube, rows, width), BF16),
        pltpu.VMEM((PARTS, *cube, rows, width), BF16),
        pltpu.VMEM((PARTS, 3, SIDE, SIDE, rows, width), BF16),
        pltpu.VMEM((PARTS, 3, SIDE, rows, width), BF16),
        pltpu.VMEM((PARTS, 3, rows, width), BF16),
        dma, dma, dma, dma,
    ]


def sae_kernel(
    rows_ref, enc_hbm, bias_ref, dec_hbm, dec_bias_ref, feat_hbm, rec_ref,
    gathered, total, planes, lines, blocks, ag_send, ag_recv, rs_send, rs_recv,
    feats, enc, dec, bias, local_sem, cross_send, cross_recv,
):
    torus = Torus()
    core, other, partner = torus.core, torus.other, torus.partner
    width = gathered.shape[-1]
    features = enc.shape[2]

    own_copies = [
        pltpu.make_async_copy(
            rows_ref.at[:, pl.ds(p * width, width)], gathered.at[(p, *torus.pos)], local_sem.at[p]
        )
        for p in range(PARTS)
    ]
    weight_copies = [
        pltpu.make_async_copy(src, dst.at[core], local_sem.at[PARTS + i])
        for i, (src, dst) in enumerate(((enc_hbm, enc), (bias_ref, bias), (dec_hbm, dec)))
    ]
    for copy in own_copies + weight_copies:
        copy.start()
    torus.meet([torus.device(axis, d) for axis in range(3) for d in OTHERS] + [partner])

    shared_copies = [
        remote(src, dst.at[core], cross_send.at[i], cross_recv.at[i], partner)
        for i, (src, dst) in enumerate(((enc_hbm, enc), (bias_ref, bias), (dec_hbm, dec)))
    ]

    def own_ready():
        for copy in own_copies:
            copy.wait()
        for copy in shared_copies:
            copy.start()

    gather = Gather(torus, lambda p: rows_ref.at[:, pl.ds(p * width, width)], gathered, ag_send, ag_recv)
    gather.run(own_ready)
    for copy in weight_copies:
        copy.wait()
    for copy in shared_copies:
        copy.wait_recv()
    def encode(step, carry):
        which, y = step // 2, 2 * lax.rem(step, 2)
        rows = 2 * SIDE * SIDE * 16
        scores = bias[which]
        for p in range(PARTS):
            block = gathered[p, pl.ds(y, 2)].reshape(rows, width)
            scores = scores + jnp.dot(
                block, enc[which, p * width : (p + 1) * width, :], preferred_element_type=F32
            )
        feats[which, pl.ds(y, 2)] = (
            jnp.maximum(scores, 0.0).astype(BF16).reshape(2, SIDE, SIDE, 16, features)
        )
        return carry

    lax.fori_loop(0, 4, encode, 0)
    own_out = pltpu.make_async_copy(feats.at[core], feat_hbm.at[:, :, :, core], local_sem.at[PARTS + 3])
    cross_out = remote(
        feats.at[other], feat_hbm.at[:, :, :, core], cross_send.at[3], cross_recv.at[3], partner
    )
    cross_in = remote(
        feats.at[other], feat_hbm.at[:, :, :, other], cross_send.at[3], cross_recv.at[3], partner
    )
    own_out.start()
    cross_out.start()

    scatter = Scatter(torus, total, planes, lines, blocks, rs_send, rs_recv)

    def produce(p, delta):
        idx = torus.index(p, (None, None, delta))
        left = [feats[(which, *idx)].reshape(SIDE * SIDE * 16, features) for which in range(2)]
        tile = 256

        def columns(step, carry):
            cols = pl.ds(pl.multiple_of(step * tile, tile), tile)
            here = pl.ds(pl.multiple_of(p * width + step * tile, tile), tile)
            value = jnp.dot(left[0], dec[0, :, here], preferred_element_type=F32) + jnp.dot(
                left[1], dec[1, :, here], preferred_element_type=F32
            )
            total[(p, *idx, ALL, cols)] = value.astype(BF16).reshape(SIDE, SIDE, 16, tile)
            return carry

        lax.fori_loop(0, width // tile, columns, 0)

    def finish(p, value):
        cols = slice(p * width, (p + 1) * width)
        rec_ref[:, cols] = value + dec_bias_ref[:, cols]

    scatter.run(produce, finish)

    own_out.wait()
    cross_out.wait_send()
    cross_in.wait_recv()
    for copy in shared_copies:
        copy.wait_send()
    gather.drain()
    scatter.drain()


def sae(rows, encoder, encoder_bias, decoder, decoder_bias):
    own_rows, model = rows.shape
    features = encoder.shape[1]
    width = model // PARTS
    cube = (SIDE, SIDE, SIDE)
    vmem = pl.BlockSpec(memory_space=pltpu.VMEM)
    hbm = pl.BlockSpec(memory_space=pl.ANY)
    dma = pltpu.SemaphoreType.DMA
    out, rec = pl.pallas_call(
        sae_kernel,
        name="sae",
        out_shape=(
            jax.ShapeDtypeStruct((*cube, 2, own_rows, features), BF16),
            jax.ShapeDtypeStruct((own_rows, model), F32),
        ),
        in_specs=[vmem, hbm, vmem, hbm, vmem],
        out_specs=(hbm, vmem),
        scratch_shapes=torus_scratch(own_rows, width)
        + [
            pltpu.VMEM((2, *cube, own_rows, features), BF16),
            pltpu.VMEM((2, model, features), BF16),
            pltpu.VMEM((2, features, model), BF16),
            pltpu.VMEM((2, 1, features), F32),
            dma((PARTS + 4,)),
            dma((4,)),
            dma((4,)),
        ],
        compiler_params=pltpu.CompilerParams(
            collective_id=0, has_side_effects=True, vmem_limit_bytes=60 * 1024 * 1024
        ),
    )(rows, encoder, encoder_bias[None, :], decoder, decoder_bias[None, :])
    return out.reshape(-1, features), rec


def moe_kernel(
    tokens_ref, meta_ref, gate_hbm, up_hbm, down_hbm, sgate_hbm, sup_hbm, sdown_hbm, out_ref,
    gate, up, down, sgate, sup, sdown, metas, partial, combine, outgoing, received, hidden, served, returned,
    parts_out, parts_in, local_sem, meta_send, meta_recv, go_send, go_recv, back_send, back_recv, part_send, part_recv,
):
    torus = Torus()
    e, f = torus.e, torus.f
    n_e, own_rows, model = outgoing.shape
    n_f = metas.shape[0]
    rows = n_f * own_rows
    slots = n_e * own_rows
    hid = hidden.shape[1]
    tile = 256

    weight_copies = [
        pltpu.make_async_copy(src, dst, local_sem.at[i])
        for i, (src, dst) in enumerate(
            (
                (sgate_hbm, sgate), (sup_hbm, sup), (sdown_hbm, sdown),
                (gate_hbm.at[0], gate), (up_hbm.at[0], up), (down_hbm.at[0], down),
            )
        )
    ]
    own_meta = pltpu.make_async_copy(meta_ref, metas.at[f], local_sem.at[6])
    for copy in weight_copies + [own_meta]:
        copy.start()

    moves = [(dy, dx) for dy in range(SIDE) for dx in range(SIDE) if dy or dx]

    def plane(dy, dx):
        return lax.rem(torus.pos[0] + dy, SIDE) * SIDE + lax.rem(torus.pos[1] + dx, SIDE)

    def column(i):
        return lax.rem(f + i, n_f)

    torus.meet([(plane(*m), f) for m in moves] + [(e, column(i)) for i in range(1, n_f)])

    sent = []

    def send(copy):
        copy.start()
        sent.append(copy)

    for i in range(1, n_f):
        send(remote(meta_ref, metas.at[f], meta_send.at[i - 1], meta_recv.at[i - 1], (e, column(i))))

    for copy in weight_copies[:3]:
        copy.wait()
    tokens = tokens_ref[...]
    shared_gate = jnp.dot(tokens, sgate[...], preferred_element_type=F32)
    shared_up = jnp.dot(tokens, sup[...], preferred_element_type=F32)
    shared_hidden = (jax.nn.silu(shared_gate) * shared_up).astype(BF16)

    own_meta.wait()
    for i in range(1, n_f):
        src = column(n_f - i)
        remote(metas.at[src], metas.at[src], meta_send.at[i - 1], meta_recv.at[i - 1], (e, src)).wait_recv()
    table = metas[...].reshape(rows, metas.shape[2])
    slot = lax.broadcasted_iota(jnp.int32, (rows, slots), 1)
    token = lax.broadcasted_iota(jnp.int32, (rows, slots), 0)
    wanted = ((slot // own_rows) * n_f + f).astype(F32)
    named = jnp.zeros((rows, slots), F32)
    weight = jnp.zeros((rows, slots), F32)
    for k in range(TOP):
        same = table[:, k : k + 1] == wanted
        named = named + jnp.where(same, 1.0, 0.0)
        weight = weight + jnp.where(same, table[:, TOP + k : TOP + k + 1], 0.0)
    row = lax.broadcasted_iota(jnp.int32, (rows, rows), 0)
    col = lax.broadcasted_iota(jnp.int32, (rows, rows), 1)
    before = jnp.where((row // own_rows == col // own_rows) & (col < row), 1.0, 0.0).astype(BF16)
    rank = jnp.dot(before, named.astype(BF16), preferred_element_type=F32)
    here = (lax.rem(slot, 2).astype(F32) == rank) & (lax.rem(slot // 2, n_f) == token // own_rows)
    places = jnp.where(here, named, 0.0)
    weight = places * weight
    high = weight.astype(BF16)
    combine[0] = high
    combine[1] = (weight - high.astype(F32)).astype(BF16)
    dispatch = places.T.astype(BF16)

    def pick(step, carry):
        cols = pl.ds(pl.multiple_of(step * tile, tile), tile)
        value = jnp.dot(dispatch, tokens_ref[:, cols], preferred_element_type=F32)
        outgoing[:, :, cols] = value.astype(BF16).reshape(n_e, own_rows, tile)
        return carry

    lax.fori_loop(0, model // tile, pick, 0)

    def exchange(src, dst, send_sem, recv_sem):
        for i, (dy, dx) in enumerate(moves):
            there = plane(dy, dx)
            send(remote(src.at[there], dst.at[e], send_sem.at[i], recv_sem.at[i], (there, f)))
        return pltpu.make_async_copy(src.at[e], dst.at[e], local_sem.at[7])

    def arrivals(dst, send_sem, recv_sem):
        for i, (dy, dx) in enumerate(moves):
            src = plane(SIDE - dy, SIDE - dx)
            remote(dst.at[src], dst.at[src], send_sem.at[i], recv_sem.at[i], (src, f)).wait_recv()

    own = exchange(outgoing, received, go_send, go_recv)
    own.start()

    def shared(step, carry):
        cols = pl.ds(pl.multiple_of(step * tile, tile), tile)
        value = jnp.dot(shared_hidden, sdown[:, cols], preferred_element_type=F32)
        partial[:, :, cols] = value.reshape(n_f, own_rows, tile)
        return carry

    lax.fori_loop(0, model // tile, shared, 0)
    for copy in weight_copies[3:]:
        copy.wait()
    own.wait()
    arrivals(received, go_send, go_recv)

    def inner(step, carry):
        cols = pl.ds(pl.multiple_of(step * tile, tile), tile)
        x = received[...].reshape(slots, model)
        gate_proj = jnp.dot(x, gate[:, cols], preferred_element_type=F32)
        up_proj = jnp.dot(x, up[:, cols], preferred_element_type=F32)
        hidden[:, cols] = (jax.nn.silu(gate_proj) * up_proj).astype(BF16)
        return carry

    lax.fori_loop(0, hid // tile, inner, 0)

    def outer(step, carry):
        cols = pl.ds(pl.multiple_of(step * tile, tile), tile)
        value = jnp.dot(hidden[...], down[:, cols], preferred_element_type=F32)
        served[:, :, cols] = value.astype(BF16).reshape(n_e, own_rows, tile)
        return carry

    lax.fori_loop(0, model // tile, outer, 0)
    own = exchange(served, returned, back_send, back_recv)
    own.start()
    own.wait()
    arrivals(returned, back_send, back_recv)

    def share(step, carry):
        cols = pl.ds(pl.multiple_of(step * tile, tile), tile)
        back = returned[:, :, cols].reshape(slots, tile)
        value = partial[:, :, cols].reshape(rows, tile)
        for i in range(2):
            value = value + jnp.dot(combine[i], back, preferred_element_type=F32)
        value = value.reshape(n_f, own_rows, tile)
        partial[:, :, cols] = value
        parts_out[:, :, cols] = value.astype(BF16)
        return carry

    lax.fori_loop(0, model // tile, share, 0)
    incoming = []
    for i in range(1, n_f):
        there = column(i)
        copy = remote(
            parts_out.at[there], parts_in.at[i - 1], part_send.at[i - 1], part_recv.at[i - 1], (e, there)
        )
        send(copy)
        incoming.append(copy)
    value = partial[f]
    for i, copy in enumerate(incoming):
        copy.wait_recv()
        value = value + parts_in[i].astype(F32)
    out_ref[...] = value.astype(BF16)
    for copy in sent:
        copy.wait_send()


def moe(tokens, meta, expert_gate, expert_up, expert_down, shared_gate, shared_up, shared_down):
    n_e, n_f = lax.axis_size("expert"), lax.axis_size("feat")
    own_rows, lanes = meta.shape
    model = tokens.shape[1]
    hid = expert_gate.shape[2]
    slots = n_e * own_rows
    vmem = pl.BlockSpec(memory_space=pltpu.VMEM)
    hbm = pl.BlockSpec(memory_space=pl.ANY)
    dma = pltpu.SemaphoreType.DMA
    weights = (expert_gate[0], expert_up[0], expert_down[0], shared_gate, shared_up, shared_down)
    return pl.pallas_call(
        moe_kernel,
        name="moe",
        out_shape=jax.ShapeDtypeStruct((own_rows, model), BF16),
        in_specs=[vmem, vmem] + [hbm] * 6,
        out_specs=vmem,
        scratch_shapes=[pltpu.VMEM(w.shape, BF16) for w in weights]
        + [
            pltpu.VMEM((n_f, own_rows, lanes), F32),
            pltpu.VMEM((n_f, own_rows, model), F32),
            pltpu.VMEM((2, n_f * own_rows, slots), BF16),
            pltpu.VMEM((n_e, own_rows, model), BF16),
            pltpu.VMEM((n_e, own_rows, model), BF16),
            pltpu.VMEM((slots, hid), BF16),
            pltpu.VMEM((n_e, own_rows, model), BF16),
            pltpu.VMEM((n_e, own_rows, model), BF16),
            pltpu.VMEM((n_f, own_rows, model), BF16),
            pltpu.VMEM((n_f - 1, own_rows, model), BF16),
            dma((8,)),
            dma((n_f - 1,)),
            dma((n_f - 1,)),
            dma((n_e - 1,)),
            dma((n_e - 1,)),
            dma((n_e - 1,)),
            dma((n_e - 1,)),
            dma((n_f - 1,)),
            dma((n_f - 1,)),
        ],
        compiler_params=pltpu.CompilerParams(
            collective_id=1, has_side_effects=True, vmem_limit_bytes=60 * 1024 * 1024
        ),
    )(tokens, meta, expert_gate, expert_up, expert_down, shared_gate, shared_up, shared_down)


def shards(
    tokens,
    expert_ids,
    gate_weights,
    expert_gate,
    expert_up,
    expert_down,
    shared_gate,
    shared_up,
    shared_down,
    encoder,
    encoder_bias,
    decoder,
    decoder_bias,
):
    meta = jnp.concatenate([expert_ids.astype(F32), gate_weights], axis=1)
    meta = jnp.pad(meta, ((0, 0), (0, 128 - meta.shape[1])))
    rows = moe(tokens, meta, expert_gate, expert_up, expert_down, shared_gate, shared_up, shared_down)
    return sae(rows, encoder, encoder_bias, decoder, decoder_bias)


def solution(mesh):
    return jax.shard_map(
        shards,
        mesh=mesh,
        in_specs=(
            P("expert", None),
            P(("expert", "feat"), None),
            P(("expert", "feat"), None),
            P(("expert", "feat"), None, None),
            P(("expert", "feat"), None, None),
            P(("expert", "feat"), None, None),
            P(None, "feat"),
            P(None, "feat"),
            P("feat", None),
            P(None, ("expert", "feat")),
            P(("expert", "feat")),
            P(("expert", "feat"), None),
            P(),
        ),
        out_specs=(P(None, ("expert", "feat")), P(("expert", "feat"), None)),
        check_vma=False,
    )
```

time: 416 us -> 139 us (0.33)
  waiting for transfers between devices: 337 us -> 0 us
  Pallas kernels: 0 us -> 131 us
  matrix products: 38.7 us -> 0 us
  starting transfers between devices: 16.6 us -> 0 us
  between operations: 13.9 us -> 0.66 us
    reduce_scatter x2 -> x0, waiting for transfers between devices: 236 us -> none  [the longest x1 236 us: shards(): lax.psum_scatter(jnp.dot(block_rows, decoder, preferred_element_type=jnp....]
    pallas_call x0 -> x2, Pallas kernels: none -> 131 us  [the longest x1 66 us: moe(): pl.pallas_call(moe_kernel, name='moe', out_shape=jax.ShapeDtypeStruct((ow...]
    all_gather x1 -> x0, waiting for transfers between devices: 65.9 us -> none  [shards(): lax.all_gather(moe_out, ('expert', 'feat'), axis=0, tiled=True)]
    dot_general x9 -> x0, matrix products: 38.7 us -> none  [the longest x1 9.09 us: shards(): jnp.dot(block_rows, decoder, preferred_element_type=jnp.float32)]
    all_to_all x2 -> x0, waiting for transfers between devices: 35.3 us -> none  [the longest x1 19 us: shards(): lax.all_to_all(served, ('expert', 'feat'), split_axis=0, concat_axis=0, t...]
    all_to_all x2 -> x0, starting transfers between devices: 16.3 us -> none  [the longest x1 11.6 us: shards(): lax.all_to_all(outgoing, ('expert', 'feat'), split_axis=0, concat_axis=0,...]
  transfers between devices with their start and end apart: 5 -> 0, of which waited for: 4 -> 0; matrix products, arithmetic and copies ran while one was open for 5% -> 0% of each run, Pallas kernels for 0% -> 0%
where the time goes in v2:
time: 139 us
  Pallas kernels  131 us (94%)
  local copies, waits for them, and re-layouts  5.89 us (4%)
    pallas_call x1, Pallas kernels, moe(): pl.pallas_call(moe_kernel, name='moe', out_shape=jax.ShapeDtypeStruct((ow...  66 us
    pallas_call x1, Pallas kernels, sae(): pl.pallas_call(sae_kernel, name='sae', out_shape=(jax.ShapeDtypeStruct((*...  65.2 us
    unnamed x5, local copies, waits for them, and re-layouts  4.5 us

profile of v2, /device:TPU:0, one launch (start us, length us, event | category | flops | bytes accessed | tf_op | source)
XLA Modules:
  0.0 139.1 jit_solution(12613738012791324857)
XLA Ops:
  0.6 0.7 convert_element_type.5
  1.3 0.1 copy.17
  1.4 0.8 copy.18
  2.2 0.7 select_maximum_fusion.meta_ref
  2.8 1.3 broadcast_in_dim.7.dec_bias_ref
  4.1 66.0 %moe.1.rows_ref = bf16[16,2304]{1,0:T(8,128)(2,1)} custom-call(bf16[128,2304]{1,0:T(8,128)(2,1)} %tokens_ref.1, f32[16,128]{1,0:T(8,128)} %select_maximum_fusion.meta_ref, bf16[1,2304,1024]{2,1,0:T(8,128)(2,1)} %gate_hbm.1, bf16[1,2304,1024]{2,1,0:T(8,128)(2,1)} %up_hbm.1, bf16[1,1024,2304]{2,1,0:T(8,128)(2,1)} %down_hbm.1, bf16[2304,128]{1,0:T(8,128)(2,1)} %sgate_hbm.1, ...), custom_call_target="tpu_custom_call" | custom-call | tf_op jit(solution)/shard_map/moe/pallas_call | solution.py:532
  70.2 65.2 %sae.1 = (bf16[4,4,4,2,16,512]{5,4,3,2,1,0:T(8,128)(2,1)}, f32[16,2304]{1,0:T(8,128)}) custom-call(bf16[16,2304]{1,0:T(8,128)(2,1)} %moe.1.rows_ref, bf16[2304,512]{1,0:T(8,128)(2,1)} %enc_hbm.1, f32[1,512]{1,0:T(1,128)} %bitcast.3, bf16[512,2304]{1,0:T(8,128)(2,1)} %dec_hbm.1, f32[1,2304]{1,0:T(1,128)} %broadcast_in_dim.7.dec_bias_ref), custom_call_target="tpu_custom_call" | custom-call | tf_op jit(solution)/shard_map/sae/pallas_call | solution.py:332
  135.4 0.0 copy-start
  135.4 3.1 %copy.21 = bf16[2048,512]{1,0:T(8,128)(2,1)} copy(bf16[2048,512]{1,0:T(8,128)(2,1)} %bitcast.2) | data formatting | bytes 4194304
  138.5 0.0 copy-done
  138.5 0.7 copy.22
Async XLA Ops:
  135.4 3.1 %copy-start = (f32[16,2304]{1,0:T(8,128)S(1)}, f32[16,2304]{1,0:T(8,128)}, u32[]{:S(2)}) copy-start(f32[16,2304]{1,0:T(8,128)} %get-tuple-element.9) | copy-start | bytes 442372

commit v3 on v2

v3 whole, which is shorter than its diff:
```python
import jax
import jax.numpy as jnp
from jax import lax
from jax.experimental import pallas as pl
from jax.experimental.pallas import tpu as pltpu
from jax.sharding import PartitionSpec as P

MESH = pl.DeviceIdType.MESH
SIDE = 4
ORDERS = ((1, 0, 2), (0, 2, 1), (2, 1, 0))
PARTS = len(ORDERS)
ALL = slice(None)
BF16 = jnp.bfloat16
F32 = jnp.float32
OUTWARD = (0, 1, -1, 2)
INWARD = (2, 1, -1, 0)
FAR_WAY = {0: 1, 2: 1, 1: -1, -1: -1}
FAR, MINUS, PLUS = 0, 1, 2
OTHERS = (1, -1, 2)
TOP = 8
COPIES = 18


class Torus:
    def __init__(self):
        self.e, self.f = lax.axis_index("expert"), lax.axis_index("feat")
        self.core = lax.rem(self.f, 2)
        self.other = 1 - self.core
        self.pos = (self.e // SIDE, lax.rem(self.e, SIDE), self.f // 2)
        self.partner = (self.e, self.f + 1 - 2 * self.core)

    def at(self, axis, delta):
        return lax.rem(self.pos[axis] + delta + SIDE, SIDE) if delta else self.pos[axis]

    def device(self, axis, delta):
        there = list(self.pos)
        there[axis] = self.at(axis, delta)
        return (there[0] * SIDE + there[1], there[2] * 2 + self.core)

    def index(self, part, offsets):
        idx = [None] * 3
        for axis, delta in zip(ORDERS[part], offsets):
            idx[axis] = ALL if delta is None else self.at(axis, delta)
        return tuple(idx)

    def meet(self, peers):
        barrier = pltpu.get_barrier_semaphore()
        for there in peers:
            pl.semaphore_signal(barrier, inc=1, device_id=there, device_id_type=MESH)
        pl.semaphore_wait(barrier, len(peers))


def remote(src, dst, send, recv, where):
    return pltpu.make_async_remote_copy(
        src_ref=src, dst_ref=dst, send_sem=send, recv_sem=recv, device_id=where, device_id_type=MESH
    )


class Gather:
    def __init__(self, torus, buf, send, recv):
        self.torus, self.buf, self.send, self.recv = torus, buf, send, recv
        self.specs = [(0, d, (0, 0, 0), (-d, 0, 0)) for d in OTHERS]
        self.specs += [(1, d, (None, 0, 0), (None, -d, 0)) for d in OTHERS]
        for d in OUTWARD:
            way = FAR_WAY[d]
            self.specs += [
                (2, 1, (None, d, 0), (None, d, -1)),
                (2, -1, (None, d, 0), (None, d, 1)),
                (2, way, (None, d, -way), (None, d, 2)),
            ]
        self.started = []

    def cells(self, part, offsets):
        return self.buf.at[(part, *self.torus.index(part, offsets))]

    def copy(self, part, k, landing):
        slot, delta, source, target = self.specs[k]
        cells = self.cells(part, target if landing else source)
        return remote(
            cells, cells, self.send.at[part, k], self.recv.at[part, k], self.torus.device(ORDERS[part][slot], delta)
        )

    def start(self, part, *ks):
        for k in ks:
            copy = self.copy(part, k, False)
            copy.start()
            self.started.append(copy)

    def wait(self, part, *ks):
        for k in ks:
            self.copy(part, k, True).wait_recv()

    def run(self, arrived):
        parts = range(PARTS)
        plane = {d: 6 + 3 * i for i, d in enumerate(OUTWARD)}
        for p in parts:
            self.wait(p, 0, 1, 2)
            self.start(p, 3, 4, 5)
        for p in parts:
            self.start(p, plane[0], plane[0] + 1)
        for i, d in enumerate((-1, 1, 2)):
            for p in parts:
                self.wait(p, 3 + i)
                self.start(p, plane[d], plane[d] + 1)
            if d == 1:
                for p in parts:
                    self.wait(p, plane[0], plane[0] + 1)
                    self.start(p, plane[0] + 2)
        for p in parts:
            arrived(p, 0)
        for d in (-1, 1, 2):
            for p in parts:
                self.wait(p, plane[d], plane[d] + 1)
                self.start(p, plane[d] + 2)
        for p in parts:
            arrived(p, -1)
            arrived(p, 1)
        for p in parts:
            for d in OUTWARD:
                self.wait(p, plane[d] + 2)
            arrived(p, 2)

    def drain(self):
        for copy in self.started:
            copy.wait_send()


class Scatter:
    def __init__(self, torus, total, planes, lines, blocks, send, recv):
        self.torus, self.total, self.send, self.recv = torus, total, send, recv
        self.specs = []
        for i, d in enumerate(INWARD):
            for way, last, kind in ((FAR_WAY[d], 2, FAR), (1, 1, MINUS), (-1, -1, PLUS)):
                self.specs.append((2, way, (None, d, last), planes, (kind, i)))
        self.specs += [(1, d, (None, d, 0), lines, (i,)) for i, d in enumerate(INWARD[:3])]
        self.specs += [(0, d, (d, 0, 0), blocks, (i,)) for i, d in enumerate(INWARD[:3])]
        self.started = []

    def cells(self, part, offsets):
        return (part, *self.torus.index(part, offsets))

    def copy(self, part, k):
        slot, delta, source, lands, place = self.specs[k]
        return remote(
            self.total.at[self.cells(part, source)],
            lands.at[(part, *place)],
            self.send.at[part, k],
            self.recv.at[part, k],
            self.torus.device(ORDERS[part][slot], delta),
        )

    def start(self, part, *ks):
        for k in ks:
            copy = self.copy(part, k)
            copy.start()
            self.started.append(copy)

    def landed(self, part, k):
        self.copy(part, k).wait_recv()
        _, _, _, lands, place = self.specs[k]
        return lands[(part, *place)].astype(F32)

    def add(self, part, offsets, ks):
        idx = self.cells(part, offsets)
        value = self.total[idx].astype(F32)
        for k in ks:
            value = value + self.landed(part, k)
        return idx, value

    def run(self, produce, finish):
        parts = range(PARTS)
        plane = {d: 3 * i for i, d in enumerate(INWARD)}

        def raw(p, way):
            for d in INWARD:
                if FAR_WAY[d] != way:
                    self.start(p, plane[d] + (1 if way == 1 else 2))

        for p in parts:
            produce(p, 2)
            self.start(p, *(plane[d] for d in INWARD))
        for p in parts:
            produce(p, 1)
            raw(p, 1)
            produce(p, -1)
            raw(p, -1)
        for p in parts:
            produce(p, 0)
        for d in INWARD:
            way = FAR_WAY[d]
            for p in parts:
                idx, value = self.add(p, (None, d, way), (plane[d],))
                self.total[idx] = value.astype(BF16)
                self.start(p, plane[d] + (1 if way == 1 else 2))
        for i, d in enumerate(INWARD):
            for p in parts:
                idx, value = self.add(p, (None, d, 0), (plane[d] + 1, plane[d] + 2))
                self.total[idx] = value.astype(BF16)
                if d:
                    self.start(p, 12 + i)
        for p in parts:
            idx, value = self.add(p, (None, 0, 0), (12, 13, 14))
            self.total[idx] = value.astype(BF16)
            self.start(p, 15, 16, 17)
        for p in parts:
            _, value = self.add(p, (0, 0, 0), (15, 16, 17))
            finish(p, value)

    def drain(self):
        for copy in self.started:
            copy.wait_send()


MOVES = (
    (2, 2), (1, 2), (3, 2), (2, 1), (2, 3), (0, 2), (2, 0), (1, 1),
    (1, 3), (3, 1), (3, 3), (0, 1), (0, 3), (1, 0), (3, 0), (0, 0),
)
HALF = len(MOVES) // 2
TILE = 256


def tiles(size, body):
    def step(i, carry):
        body(pl.ds(pl.multiple_of(i * TILE, TILE), TILE))
        return carry

    lax.fori_loop(0, size // TILE, step, 0)


def layer_kernel(
    tokens_ref, ids_ref, weights_ref, gate_hbm, up_hbm, down_hbm, sgate_hbm, sup_hbm, sdown_hbm,
    enc_hbm, bias_ref, dec_hbm, feat_hbm, rec_ref,
    gate, up, down, sgate, sup, sdown, meta, metas, partial, combine, outgoing, received, hidden, served, returned,
    parts_out, parts_in, gathered, total, planes, lines, blocks, scores, feats, enc, dec, bias,
    local_sem, meta_send, meta_recv, go_send, go_recv, back_send, back_recv, part_send, part_recv,
    ag_send, ag_recv, rs_send, rs_recv, cross_send, cross_recv,
):
    torus = Torus()
    e, f, core, other, partner = torus.e, torus.f, torus.core, torus.other, torus.partner
    n_e, own_rows, model = outgoing.shape
    n_f = metas.shape[0]
    rows = n_f * own_rows
    slots = n_e * own_rows
    chunk = HALF * own_rows
    width = gathered.shape[-1]
    features = enc.shape[2]

    weight_copies = [
        pltpu.make_async_copy(src, dst, local_sem.at[i])
        for i, (src, dst) in enumerate(
            (
                (sgate_hbm, sgate), (sup_hbm, sup), (sdown_hbm, sdown),
                (gate_hbm.at[0], gate), (up_hbm.at[0], up), (down_hbm.at[0], down),
                (enc_hbm, enc.at[core]), (bias_ref, bias.at[core]), (dec_hbm, dec.at[core]),
            )
        )
    ]
    for copy in weight_copies:
        copy.start()
    own_sem, feat_sem = local_sem.at[9], local_sem.at[10]

    meta[...] = jnp.zeros_like(meta)
    meta[:TOP, :own_rows] = ids_ref[...].astype(F32)
    meta[TOP:, :own_rows] = weights_ref[...]
    metas[f] = meta[...]

    def plane(move, sign=1):
        dy, dx = move
        y = lax.rem(torus.pos[0] + SIDE + sign * dy, SIDE)
        return y * SIDE + lax.rem(torus.pos[1] + SIDE + sign * dx, SIDE)

    def column(i):
        return lax.rem(f + i, n_f)

    torus.meet(
        [(plane(m), f) for m in MOVES[:-1]]
        + [(e, column(i)) for i in range(1, n_f)]
    )
    sent = []

    def send(copy):
        copy.start()
        sent.append(copy)

    for i in range(1, n_f):
        send(remote(meta, metas.at[f], meta_send.at[i - 1], meta_recv.at[i - 1], (e, column(i))))

    for copy in weight_copies[:3]:
        copy.wait()
    tokens = tokens_ref[...]
    shared_gate = jnp.dot(tokens, sgate[...], preferred_element_type=F32)
    shared_up = jnp.dot(tokens, sup[...], preferred_element_type=F32)
    shared_hidden = (jax.nn.silu(shared_gate) * shared_up).astype(BF16)

    for i in range(1, n_f):
        src = column(n_f - i)
        remote(metas.at[src], metas.at[src], meta_send.at[i - 1], meta_recv.at[i - 1], (e, src)).wait_recv()
    turned = metas[...].reshape(rows, metas.shape[2]).T[:own_rows]
    table = jnp.concatenate(
        [turned] + [pltpu.roll(turned, rows - own_rows * i, 1) for i in range(1, n_f)], axis=0
    )
    slot = lax.broadcasted_iota(jnp.int32, (rows, slots), 1)
    token = lax.broadcasted_iota(jnp.int32, (rows, slots), 0)
    column_slot = lax.broadcasted_iota(jnp.int32, (1, slots), 1) // own_rows
    wanted = jnp.zeros((1, slots), jnp.int32)
    for i, move in enumerate(MOVES):
        wanted = jnp.where(column_slot == i, plane(move) * n_f + f, wanted)
    wanted = wanted.astype(F32)
    named = jnp.zeros((rows, slots), F32)
    weight = jnp.zeros((rows, slots), F32)
    for k in range(TOP):
        same = table[:, k : k + 1] == wanted
        named = named + jnp.where(same, 1.0, 0.0)
        weight = weight + jnp.where(same, table[:, TOP + k : TOP + k + 1], 0.0)
    row = lax.broadcasted_iota(jnp.int32, (rows, rows), 0)
    col = lax.broadcasted_iota(jnp.int32, (rows, rows), 1)
    before = jnp.where((row // own_rows == col // own_rows) & (col < row), 1.0, 0.0).astype(BF16)
    rank = jnp.dot(before, named.astype(BF16), preferred_element_type=F32)
    here = (lax.rem(slot, 2).astype(F32) == rank) & (lax.rem(slot // 2, n_f) == token // own_rows)
    places = jnp.where(here, named, 0.0)
    weight = places * weight
    high = weight.astype(BF16)
    combine[0] = high
    combine[1] = (weight - high.astype(F32)).astype(BF16)
    dispatch = places.T.astype(BF16)

    halves = (range(HALF), range(HALF, n_e))

    def span(half):
        return slice(half * HALF, (half + 1) * HALF)

    def exchange(src, dst, send_sem, recv_sem, half):
        for i in halves[half]:
            if i < n_e - 1:
                send(remote(src.at[i], dst.at[i], send_sem.at[i], recv_sem.at[i], (plane(MOVES[i]), f)))
            else:
                copy = pltpu.make_async_copy(src.at[i], dst.at[i], own_sem)
                copy.start()

    def arrivals(src, dst, send_sem, recv_sem, half):
        for i in halves[half]:
            if i < n_e - 1:
                remote(
                    src.at[i], dst.at[i], send_sem.at[i], recv_sem.at[i], (plane(MOVES[i], -1), f)
                ).wait_recv()
            else:
                pltpu.make_async_copy(src.at[i], dst.at[i], own_sem).wait()

    for half in range(2):
        mine = dispatch[half * chunk : (half + 1) * chunk]

        def pick(cols, half=half, mine=mine):
            value = jnp.dot(mine, tokens_ref[:, cols], preferred_element_type=F32)
            outgoing[span(half), :, cols] = value.astype(BF16).reshape(HALF, own_rows, TILE)

        tiles(model, pick)
        exchange(outgoing, received, go_send, go_recv, half)

    for copy in weight_copies[6:]:
        copy.wait()
    cross_copies = [
        remote(ref.at[core], ref.at[core], cross_send.at[i], cross_recv.at[i], partner)
        for i, ref in enumerate((enc, bias, dec))
    ]
    for copy in cross_copies:
        send(copy)

    def shared(cols):
        value = jnp.dot(shared_hidden, sdown[:, cols], preferred_element_type=F32)
        partial[:, :, cols] = value.reshape(n_f, own_rows, TILE)

    tiles(model, shared)
    for copy in weight_copies[3:6]:
        copy.wait()

    for half in range(2):
        arrivals(outgoing, received, go_send, go_recv, half)

        def inner(cols, half=half):
            x = received[span(half)].reshape(chunk, model)
            gate_proj = jnp.dot(x, gate[:, cols], preferred_element_type=F32)
            up_proj = jnp.dot(x, up[:, cols], preferred_element_type=F32)
            hidden[:, cols] = (jax.nn.silu(gate_proj) * up_proj).astype(BF16)

        tiles(hidden.shape[1], inner)

        def outer(cols, half=half):
            value = jnp.dot(hidden[...], down[:, cols], preferred_element_type=F32)
            served[span(half), :, cols] = value.astype(BF16).reshape(HALF, own_rows, TILE)

        tiles(model, outer)
        for i in halves[half]:
            if i < n_e - 1:
                send(
                    remote(
                        served.at[i], returned.at[i], back_send.at[i], back_recv.at[i], (plane(MOVES[i], -1), f)
                    )
                )
            else:
                pltpu.make_async_copy(served.at[i], returned.at[i], own_sem).start()

    def summed(cols, half):
        back = returned[span(half), :, cols].reshape(chunk, TILE)
        value = partial[:, :, cols].reshape(rows, TILE)
        for i in range(2):
            value = value + jnp.dot(
                combine[i, :, half * chunk : (half + 1) * chunk], back, preferred_element_type=F32
            )
        value = value.reshape(n_f, own_rows, TILE)
        partial[:, :, cols] = value
        return value

    def returns(half):
        for i in halves[half]:
            if i < n_e - 1:
                remote(
                    served.at[i], returned.at[i], back_send.at[i], back_recv.at[i], (plane(MOVES[i]), f)
                ).wait_recv()
            else:
                pltpu.make_async_copy(served.at[i], returned.at[i], own_sem).wait()

    def fill(y, carry):
        for which in range(2):
            scores[which, y] = jnp.broadcast_to(bias[which], (SIDE, SIDE, own_rows, features))
        return carry

    for copy in cross_copies:
        copy.wait_recv()
    lax.fori_loop(0, SIDE, fill, 0)

    def share_far(cols):
        summed(cols, 0)

    returns(0)
    tiles(model, share_far)
    returns(1)
    incoming = {}
    for p in range(PARTS):

        def share_near(i, carry, p=p):
            cols = pl.ds(pl.multiple_of(p * width + i * TILE, TILE), TILE)
            parts_out[:, :, cols] = summed(cols, 1).astype(BF16)
            return carry

        lax.fori_loop(0, width // TILE, share_near, 0)
        cols = pl.ds(p * width, width)
        for i in range(1, n_f):
            there = column(i)
            copy = remote(
                parts_out.at[there, :, cols], parts_in.at[i - 1, :, cols],
                part_send.at[p, i - 1], part_recv.at[p, i - 1], (e, there),
            )
            send(copy)
            incoming[p, i] = copy

    gather = Gather(torus, gathered, ag_send, ag_recv)
    for p in range(PARTS):
        cols = pl.ds(p * width, width)
        value = partial[f, :, cols]
        for i in range(1, n_f):
            incoming[p, i].wait_recv()
            value = value + parts_in[i - 1, :, cols].astype(F32)
        gathered[(p, *torus.pos)] = value.astype(BF16)
        gather.start(p, 0, 1, 2)

    def encode(p, delta):
        idx = torus.index(p, (None, None, delta))

        def step(i, carry):
            which = i // (features // TILE)
            cols = pl.ds(pl.multiple_of(lax.rem(i, features // TILE) * TILE, TILE), TILE)
            block = gathered[(p, *idx)].reshape(SIDE * SIDE * own_rows, width)
            value = jnp.dot(block, enc[which, p * width : (p + 1) * width, cols], preferred_element_type=F32)
            at = (which, *idx, ALL, cols)
            scores[at] = scores[at] + value.reshape(SIDE, SIDE, own_rows, TILE)
            return carry

        lax.fori_loop(0, 2 * features // TILE, step, 0)

    gather.run(encode)

    def rectify(y, carry):
        for which in range(2):
            feats[which, y] = jnp.maximum(scores[which, y], 0.0).astype(BF16)
        return carry

    lax.fori_loop(0, SIDE, rectify, 0)
    own_out = pltpu.make_async_copy(feats.at[core], feat_hbm.at[:, :, :, core], feat_sem)
    cross_out = remote(
        feats.at[other], feat_hbm.at[:, :, :, core], cross_send.at[3], cross_recv.at[3], partner
    )
    cross_in = remote(
        feats.at[other], feat_hbm.at[:, :, :, other], cross_send.at[3], cross_recv.at[3], partner
    )
    own_out.start()
    cross_out.start()

    scatter = Scatter(torus, total, planes, lines, blocks, rs_send, rs_recv)

    def produce(p, delta):
        idx = torus.index(p, (None, None, delta))
        left = [feats[(which, *idx)].reshape(SIDE * SIDE * own_rows, features) for which in range(2)]

        def step(i, carry):
            cols = pl.ds(pl.multiple_of(i * TILE, TILE), TILE)
            here = pl.ds(pl.multiple_of(p * width + i * TILE, TILE), TILE)
            value = jnp.dot(left[0], dec[0, :, here], preferred_element_type=F32) + jnp.dot(
                left[1], dec[1, :, here], preferred_element_type=F32
            )
            total[(p, *idx, ALL, cols)] = value.astype(BF16).reshape(SIDE, SIDE, own_rows, TILE)
            return carry

        lax.fori_loop(0, width // TILE, step, 0)

    def finish(p, value):
        rec_ref[:, p * width : (p + 1) * width] = value

    scatter.run(produce, finish)

    own_out.wait()
    cross_out.wait_send()
    cross_in.wait_recv()
    for copy in sent:
        copy.wait_send()
    gather.drain()
    scatter.drain()


def layer(tokens, ids, weights, routed, shared, encoder, encoder_bias, decoder):
    n_e, n_f = lax.axis_size("expert"), lax.axis_size("feat")
    own_rows = ids.shape[1]
    model = tokens.shape[1]
    hid = routed[0].shape[2]
    slots = n_e * own_rows
    rows = n_f * own_rows
    features = encoder.shape[1]
    width = model // PARTS
    cube = (SIDE, SIDE, SIDE)
    vmem = pl.BlockSpec(memory_space=pltpu.VMEM)
    hbm = pl.BlockSpec(memory_space=pl.ANY)
    dma = pltpu.SemaphoreType.DMA
    plane_rows = pltpu.VMEM((n_e, own_rows, model), BF16)
    torus_sem = dma((PARTS, COPIES))
    return pl.pallas_call(
        layer_kernel,
        name="layer",
        out_shape=(
            jax.ShapeDtypeStruct((*cube, 2, own_rows, features), BF16),
            jax.ShapeDtypeStruct((own_rows, model), F32),
        ),
        in_specs=[vmem] * 3 + [hbm] * 7 + [vmem, hbm],
        out_specs=(hbm, vmem),
        scratch_shapes=[pltpu.VMEM(w.shape[1:], BF16) for w in routed]
        + [pltpu.VMEM(w.shape, BF16) for w in shared]
        + [
            pltpu.VMEM((2 * TOP, rows), F32),
            pltpu.VMEM((n_f, 2 * TOP, rows), F32),
            pltpu.VMEM((n_f, own_rows, model), F32),
            pltpu.VMEM((2, rows, slots), BF16),
            plane_rows,
            plane_rows,
            pltpu.VMEM((HALF * own_rows, hid), BF16),
            plane_rows,
            plane_rows,
            pltpu.VMEM((n_f, own_rows, model), BF16),
            pltpu.VMEM((n_f - 1, own_rows, model), BF16),
            pltpu.VMEM((PARTS, *cube, own_rows, width), BF16),
            pltpu.VMEM((PARTS, *cube, own_rows, width), BF16),
            pltpu.VMEM((PARTS, 3, SIDE, SIDE, own_rows, width), BF16),
            pltpu.VMEM((PARTS, 3, SIDE, own_rows, width), BF16),
            pltpu.VMEM((PARTS, 3, own_rows, width), BF16),
            pltpu.VMEM((2, *cube, own_rows, features), F32),
            pltpu.VMEM((2, *cube, own_rows, features), BF16),
            pltpu.VMEM((2, model, features), BF16),
            pltpu.VMEM((2, features, model), BF16),
            pltpu.VMEM((2, 1, features), F32),
            dma((11,)),
            dma((n_f - 1,)),
            dma((n_f - 1,)),
            dma((n_e - 1,)),
            dma((n_e - 1,)),
            dma((n_e - 1,)),
            dma((n_e - 1,)),
            dma((PARTS, n_f - 1)),
            dma((PARTS, n_f - 1)),
            torus_sem, torus_sem, torus_sem, torus_sem,
            dma((4,)),
            dma((4,)),
        ],
        compiler_params=pltpu.CompilerParams(
            collective_id=0, has_side_effects=True, vmem_limit_bytes=63 * 1024 * 1024
        ),
    )(tokens, ids, weights, *routed, *shared, encoder, encoder_bias, decoder)


def shards(
    tokens,
    expert_ids,
    gate_weights,
    expert_gate,
    expert_up,
    expert_down,
    shared_gate,
    shared_up,
    shared_down,
    encoder,
    encoder_bias,
    decoder,
    decoder_bias,
):
    features, sums = layer(
        tokens,
        expert_ids.T,
        gate_weights.T,
        (expert_gate, expert_up, expert_down),
        (shared_gate, shared_up, shared_down),
        encoder,
        encoder_bias[None, :],
        decoder,
    )
    return features.reshape(-1, encoder.shape[1]), sums + decoder_bias[None, :]


def solution(mesh):
    return jax.shard_map(
        shards,
        mesh=mesh,
        in_specs=(
            P("expert", None),
            P(("expert", "feat"), None),
            P(("expert", "feat"), None),
            P(("expert", "feat"), None, None),
            P(("expert", "feat"), None, None),
            P(("expert", "feat"), None, None),
            P(None, "feat"),
            P(None, "feat"),
            P("feat", None),
            P(None, ("expert", "feat")),
            P(("expert", "feat")),
            P(("expert", "feat"), None),
            P(),
        ),
        out_specs=(P(None, ("expert", "feat")), P(("expert", "feat"), None)),
        check_vma=False,
    )
```

time: 139 us -> 123 us (0.88)
  Pallas kernels: 131 us -> 118 us
  local copies, waits for them, and re-layouts: 5.89 us -> 3.05 us
    pallas_call x2 -> x1, Pallas kernels: 131 us -> 118 us  [layer(): pl.pallas_call(layer_kernel, name='layer', out_shape=(jax.ShapeDtypeStruc...]
    add x0 -> x1, other arithmetic: none -> 1.58 us  [shards(): sums + decoder_bias[None, :]]
    unnamed x5 -> x3, local copies, waits for them, and re-layouts: 4.5 us -> 3.05 us
where the time goes in v3:
time: 123 us
  Pallas kernels  118 us (96%)
  local copies, waits for them, and re-layouts  3.05 us (2%)
  other arithmetic  1.58 us (1%)
    pallas_call x1, Pallas kernels, layer(): pl.pallas_call(layer_kernel, name='layer', out_shape=(jax.ShapeDtypeStruc...  118 us
    unnamed x3, local copies, waits for them, and re-layouts  3.05 us

profile of v3, /device:TPU:0, one launch (start us, length us, event | category | flops | bytes accessed | tf_op | source)
XLA Modules:
  0.0 123.2 jit_solution(10990168659208790869)
XLA Ops:
  0.6 0.0 copy-start
  0.6 117.9 %layer.1 = (bf16[4,4,4,2,16,512]{5,4,3,2,1,0:T(8,128)(2,1)}, f32[16,2304]{1,0:T(8,128)}) custom-call(bf16[128,2304]{1,0:T(8,128)(2,1)} %tokens_ref.1, s32[8,16]{1,0:T(8,128)} %bitcast.5, f32[8,16]{1,0:T(8,128)} %bitcast.6, bf16[1,2304,1024]{2,1,0:T(8,128)(2,1)} %gate_hbm.1, bf16[1,2304,1024]{2,1,0:T(8,128)(2,1)} %up_hbm.1, bf16[1,1024,2304]{2,1,0:T(8,128)(2,1)} %down_hbm.1, ...), custom_call_target="tpu_custom_call" | custom-call | tf_op jit(solution)/shard_map/layer/pallas_call | solution.py:544
  118.6 0.0 copy-done
  118.6 1.6 %broadcast_add_fusion = f32[16,2304]{1,0:T(8,128)} fusion(f32[16,2304]{1,0:T(8,128)} %get-tuple-element.5, f32[2304]{0:T(1024)S(1)} %copy-done), kind=kLoop, calls=%fused_computation | loop fusion | flops 36864 | bytes 304128 | tf_op jit(solution)/shard_map/add | solution.py:621
  120.2 3.0 %copy.16 = bf16[2048,512]{1,0:T(8,128)(2,1)} copy(bf16[2048,512]{1,0:T(8,128)(2,1)} %bitcast.4) | data formatting | bytes 4194304
Async XLA Ops:
  0.6 117.9 %copy-start = (f32[2304]{0:T(1024)S(1)}, f32[2304]{0:T(1024)}, u32[]{:S(2)}) copy-start(f32[2304]{0:T(1024)} %param.25) | copy-start | bytes 27652

commit v4 on v3

--- a/solution.py
+++ b/solution.py
@@ -1,3 +1,5 @@
+import functools
+
 import jax
 import jax.numpy as jnp
 from jax import lax
@@ -90,35 +92,40 @@
         for k in ks:
             self.copy(part, k, True).wait_recv()
 
-    def run(self, arrived):
-        parts = range(PARTS)
+    def steps(self, p, arrived):
         plane = {d: 6 + 3 * i for i, d in enumerate(OUTWARD)}
-        for p in parts:
+
+        def go_on(d):
+            self.wait(p, plane[d], plane[d] + 1)
+            self.start(p, plane[d] + 2)
+
+        def lines():
             self.wait(p, 0, 1, 2)
-            self.start(p, 3, 4, 5)
-        for p in parts:
-            self.start(p, plane[0], plane[0] + 1)
-        for i, d in enumerate((-1, 1, 2)):
-            for p in parts:
-                self.wait(p, 3 + i)
+            self.start(p, 3, 4, 5, plane[0], plane[0] + 1)
+
+        def near_planes():
+            for k, d in ((3, -1), (4, 1)):
+                self.wait(p, k)
                 self.start(p, plane[d], plane[d] + 1)
-            if d == 1:
-                for p in parts:
-                    self.wait(p, plane[0], plane[0] + 1)
-                    self.start(p, plane[0] + 2)
-        for p in parts:
+            go_on(0)
+
+        def far_planes():
+            self.wait(p, 5)
+            self.start(p, plane[2], plane[2] + 1)
             arrived(p, 0)
-        for d in (-1, 1, 2):
-            for p in parts:
-                self.wait(p, plane[d], plane[d] + 1)
-                self.start(p, plane[d] + 2)
-        for p in parts:
+
+        def far_near():
+            go_on(-1)
+            go_on(1)
+            go_on(2)
+
+        def last():
             arrived(p, -1)
             arrived(p, 1)
-        for p in parts:
-            for d in OUTWARD:
-                self.wait(p, plane[d] + 2)
+            self.wait(p, *(plane[d] + 2 for d in OUTWARD))
             arrived(p, 2)
+
+        return lines, near_planes, far_planes, far_near, last
 
     def drain(self):
         for copy in self.started:
@@ -257,7 +264,7 @@
     ]
     for copy in weight_copies:
         copy.start()
-    own_sem, feat_sem = local_sem.at[9], local_sem.at[10]
+    feat_sem = local_sem.at[9]
 
     meta[...] = jnp.zeros_like(meta)
     meta[:TOP, :own_rows] = ids_ref[...].astype(F32)
@@ -324,37 +331,24 @@
     combine[1] = (weight - high.astype(F32)).astype(BF16)
     dispatch = places.T.astype(BF16)
 
-    halves = (range(HALF), range(HALF, n_e))
+    halves = (range(HALF), range(HALF, n_e - 1))
 
     def span(half):
         return slice(half * HALF, (half + 1) * HALF)
 
-    def exchange(src, dst, send_sem, recv_sem, half):
-        for i in halves[half]:
-            if i < n_e - 1:
-                send(remote(src.at[i], dst.at[i], send_sem.at[i], recv_sem.at[i], (plane(MOVES[i]), f)))
-            else:
-                copy = pltpu.make_async_copy(src.at[i], dst.at[i], own_sem)
-                copy.start()
-
-    def arrivals(src, dst, send_sem, recv_sem, half):
-        for i in halves[half]:
-            if i < n_e - 1:
-                remote(
-                    src.at[i], dst.at[i], send_sem.at[i], recv_sem.at[i], (plane(MOVES[i], -1), f)
-                ).wait_recv()
-            else:
-                pltpu.make_async_copy(src.at[i], dst.at[i], own_sem).wait()
-
     for half in range(2):
         mine = dispatch[half * chunk : (half + 1) * chunk]
 
         def pick(cols, half=half, mine=mine):
             value = jnp.dot(mine, tokens_ref[:, cols], preferred_element_type=F32)
-            outgoing[span(half), :, cols] = value.astype(BF16).reshape(HALF, own_rows, TILE)
+            value = value.astype(BF16).reshape(HALF, own_rows, TILE)
+            outgoing[span(half), :, cols] = value
+            if half:
+                received[n_e - 1, :, cols] = value[HALF - 1]
 
         tiles(model, pick)
-        exchange(outgoing, received, go_send, go_recv, half)
+        for i in halves[half]:
+            send(remote(outgoing.at[i], received.at[i], go_send.at[i], go_recv.at[i], (plane(MOVES[i]), f)))
 
     for copy in weight_copies[6:]:
         copy.wait()
@@ -374,50 +368,43 @@
         copy.wait()
 
     for half in range(2):
-        arrivals(outgoing, received, go_send, go_recv, half)
+        for i in halves[half]:
+            remote(
+                outgoing.at[i], received.at[i], go_send.at[i], go_recv.at[i], (plane(MOVES[i], -1), f)
+            ).wait_recv()
 
         def inner(cols, half=half):
             x = received[span(half)].reshape(chunk, model)
             gate_proj = jnp.dot(x, gate[:, cols], preferred_element_type=F32)
             up_proj = jnp.dot(x, up[:, cols], preferred_element_type=F32)
-            hidden[:, cols] = (jax.nn.silu(gate_proj) * up_proj).astype(BF16)
-
-        tiles(hidden.shape[1], inner)
-
-        def outer(cols, half=half):
-            value = jnp.dot(hidden[...], down[:, cols], preferred_element_type=F32)
-            served[span(half), :, cols] = value.astype(BF16).reshape(HALF, own_rows, TILE)
-
-        tiles(model, outer)
-        for i in halves[half]:
-            if i < n_e - 1:
-                send(
-                    remote(
-                        served.at[i], returned.at[i], back_send.at[i], back_recv.at[i], (plane(MOVES[i], -1), f)
-                    )
-                )
-            else:
-                pltpu.make_async_copy(served.at[i], returned.at[i], own_sem).start()
-
-    def summed(cols, half):
-        back = returned[span(half), :, cols].reshape(chunk, TILE)
-        value = partial[:, :, cols].reshape(rows, TILE)
-        for i in range(2):
-            value = value + jnp.dot(
-                combine[i, :, half * chunk : (half + 1) * chunk], back, preferred_element_type=F32
-            )
-        value = value.reshape(n_f, own_rows, TILE)
-        partial[:, :, cols] = value
-        return value
-
-    def returns(half):
-        for i in halves[half]:
-            if i < n_e - 1:
-                remote(
-                    served.at[i], returned.at[i], back_send.at[i], back_recv.at[i], (plane(MOVES[i]), f)
-                ).wait_recv()
-            else:
-                pltpu.make_async_copy(served.at[i], returned.at[i], own_sem).wait()
+            hidden[half, :, cols] = (jax.nn.silu(gate_proj) * up_proj).astype(BF16)
+
+        tiles(hidden.shape[2], inner)
+
+    def part_tiles(p, body):
+        def step(i, carry):
+            body(pl.ds(pl.multiple_of(p * width + i * TILE, TILE), TILE))
+            return carry
+
+        lax.fori_loop(0, width // TILE, step, 0)
+
+    def back_copy(p, i, sign):
+        cols = pl.ds(p * width, width)
+        return remote(
+            served.at[i, :, cols], returned.at[i, :, cols],
+            back_send.at[p, i], back_recv.at[p, i], (plane(MOVES[i], sign), f),
+        )
+
+    def outer(cols):
+        value = jnp.dot(hidden[...].reshape(slots, hidden.shape[2]), down[:, cols], preferred_element_type=F32)
+        value = value.astype(BF16).reshape(n_e, own_rows, TILE)
+        served[:, :, cols] = value
+        returned[n_e - 1, :, cols] = value[n_e - 1]
+
+    for p in range(PARTS):
+        part_tiles(p, outer)
+        for i in range(n_e - 1):
+            send(back_copy(p, i, -1))
 
     def fill(y, carry):
         for which in range(2):
@@ -428,21 +415,22 @@
         copy.wait_recv()
     lax.fori_loop(0, SIDE, fill, 0)
 
-    def share_far(cols):
-        summed(cols, 0)
-
-    returns(0)
-    tiles(model, share_far)
-    returns(1)
+    gather = Gather(torus, gathered, ag_send, ag_recv)
     incoming = {}
-    for p in range(PARTS):
-
-        def share_near(i, carry, p=p):
-            cols = pl.ds(pl.multiple_of(p * width + i * TILE, TILE), TILE)
-            parts_out[:, :, cols] = summed(cols, 1).astype(BF16)
-            return carry
-
-        lax.fori_loop(0, width // TILE, share_near, 0)
+
+    def share(cols):
+        back = returned[:, :, cols].reshape(slots, TILE)
+        value = partial[:, :, cols].reshape(rows, TILE)
+        for i in range(2):
+            value = value + jnp.dot(combine[i], back, preferred_element_type=F32)
+        value = value.reshape(n_f, own_rows, TILE)
+        partial[:, :, cols] = value
+        parts_out[:, :, cols] = value.astype(BF16)
+
+    def give(p):
+        for i in range(n_e - 1):
+            back_copy(p, i, 1).wait_recv()
+        part_tiles(p, share)
         cols = pl.ds(p * width, width)
         for i in range(1, n_f):
             there = column(i)
@@ -453,8 +441,7 @@
             send(copy)
             incoming[p, i] = copy
 
-    gather = Gather(torus, gathered, ag_send, ag_recv)
-    for p in range(PARTS):
+    def take(p):
         cols = pl.ds(p * width, width)
         value = partial[f, :, cols]
         for i in range(1, n_f):
@@ -477,7 +464,13 @@
 
         lax.fori_loop(0, 2 * features // TILE, step, 0)
 
-    gather.run(encode)
+    steps = [
+        [functools.partial(give, p), functools.partial(take, p), *gather.steps(p, encode)] for p in range(PARTS)
+    ]
+    for turn in range(len(steps[0]) + PARTS - 1):
+        for p in reversed(range(PARTS)):
+            if 0 <= turn - p < len(steps[p]):
+                steps[p][turn - p]()
 
     def rectify(y, carry):
         for which in range(2):
@@ -559,7 +552,7 @@
             pltpu.VMEM((2, rows, slots), BF16),
             plane_rows,
             plane_rows,
-            pltpu.VMEM((HALF * own_rows, hid), BF16),
+            pltpu.VMEM((2, HALF * own_rows, hid), BF16),
             plane_rows,
             plane_rows,
             pltpu.VMEM((n_f, own_rows, model), BF16),
@@ -574,13 +567,13 @@
             pltpu.VMEM((2, model, features), BF16),
             pltpu.VMEM((2, features, model), BF16),
             pltpu.VMEM((2, 1, features), F32),
-            dma((11,)),
+            dma((10,)),
             dma((n_f - 1,)),
             dma((n_f - 1,)),
             dma((n_e - 1,)),
             dma((n_e - 1,)),
-            dma((n_e - 1,)),
-            dma((n_e - 1,)),
+            dma((PARTS, n_e - 1)),
+            dma((PARTS, n_e - 1)),
             dma((PARTS, n_f - 1)),
             dma((PARTS, n_f - 1)),
             torus_sem, torus_sem, torus_sem, torus_sem,
@@ -591,6 +584,43 @@
             collective_id=0, has_side_effects=True, vmem_limit_bytes=63 * 1024 * 1024
         ),
     )(tokens, ids, weights, *routed, *shared, encoder, encoder_bias, decoder)
+
+
+def finish_kernel(feat_hbm, sums_ref, bias_ref, out_hbm, rec_ref, held, in_sem, out_sem):
+    reads = [pltpu.make_async_copy(feat_hbm.at[y], held.at[y], in_sem.at[y]) for y in range(SIDE)]
+    writes = [pltpu.make_async_copy(held.at[y], out_hbm.at[y], out_sem.at[y]) for y in range(SIDE)]
+    for copy in reads:
+        copy.start()
+    lanes = bias_ref.shape[1]
+    for i in range(bias_ref.shape[0]):
+        cols = slice(i * lanes, (i + 1) * lanes)
+        rec_ref[:, cols] = sums_ref[:, cols] + bias_ref[i : i + 1, :]
+    for y in range(SIDE):
+        reads[y].wait()
+        writes[y].start()
+    for copy in writes:
+        copy.wait()
+
+
+def finish(features, sums, bias):
+    vmem = pl.BlockSpec(memory_space=pltpu.VMEM)
+    hbm = pl.BlockSpec(memory_space=pl.ANY)
+    return pl.pallas_call(
+        finish_kernel,
+        name="finish",
+        out_shape=(
+            jax.ShapeDtypeStruct(features.shape, features.dtype),
+            jax.ShapeDtypeStruct(sums.shape, sums.dtype),
+        ),
+        in_specs=[hbm, vmem, vmem],
+        out_specs=(hbm, vmem),
+        scratch_shapes=[
+            pltpu.VMEM(features.shape, features.dtype),
+            pltpu.SemaphoreType.DMA((SIDE,)),
+            pltpu.SemaphoreType.DMA((SIDE,)),
+        ],
+        compiler_params=pltpu.CompilerParams(vmem_limit_bytes=60 * 1024 * 1024),
+    )(features, sums, bias.reshape(-1, 128))
 
 
 def shards(
@@ -618,7 +648,8 @@
         encoder_bias[None, :],
         decoder,
     )
-    return features.reshape(-1, encoder.shape[1]), sums + decoder_bias[None, :]
+    features, sums = finish(features, sums, decoder_bias)
+    return features.reshape(-1, encoder.shape[1]), sums
 
 
 def solution(mesh):

time: 123 us -> 121 us (0.984)
  local copies, waits for them, and re-layouts: 3.05 us -> 0 us
  Pallas kernels: 118 us -> 121 us
  other arithmetic: 1.58 us -> 0 us
    pallas_call x0 -> x1, Pallas kernels: none -> 3.99 us  [finish(): pl.pallas_call(finish_kernel, name='finish', out_shape=(jax.ShapeDtypeStr...]
    unnamed x3 -> x0, local copies, waits for them, and re-layouts: 3.05 us -> none
    add x1 -> x0, other arithmetic: 1.58 us -> none  [shards(): sums + decoder_bias[None, :]]
    pallas_call x1, Pallas kernels: 118 us -> 117 us  [layer(): pl.pallas_call(layer_kernel, name='layer', out_shape=(jax.ShapeDtypeStruc...]
where the time goes in v4:
time: 121 us
  Pallas kernels  121 us (100%)
    pallas_call x1, Pallas kernels, layer(): pl.pallas_call(layer_kernel, name='layer', out_shape=(jax.ShapeDtypeStruc...  117 us
    pallas_call x1, Pallas kernels, finish(): pl.pallas_call(finish_kernel, name='finish', out_shape=(jax.ShapeDtypeStr...  3.99 us

profile of v4, /device:TPU:0, one launch (start us, length us, event | category | flops | bytes accessed | tf_op | source)
XLA Modules:
  0.0 121.3 jit_solution(6734771867772516720)
XLA Ops:
  0.6 116.6 %layer.1 = (bf16[4,4,4,2,16,512]{5,4,3,2,1,0:T(8,128)(2,1)}, f32[16,2304]{1,0:T(8,128)}) custom-call(bf16[128,2304]{1,0:T(8,128)(2,1)} %tokens_ref.1, s32[8,16]{1,0:T(8,128)} %bitcast.6, f32[8,16]{1,0:T(8,128)} %bitcast.7, bf16[1,2304,1024]{2,1,0:T(8,128)(2,1)} %gate_hbm.1, bf16[1,2304,1024]{2,1,0:T(8,128)(2,1)} %up_hbm.1, bf16[1,1024,2304]{2,1,0:T(8,128)(2,1)} %down_hbm.1, ...), custom_call_target="tpu_custom_call" | custom-call | tf_op jit(solution)/shard_map/layer/pallas_call | solution.py:537
  117.3 4.0 %finish.1 = (bf16[4,4,4,2,16,512]{5,4,3,2,1,0:T(8,128)(2,1)}, f32[16,2304]{1,0:T(8,128)}) custom-call(bf16[4,4,4,2,16,512]{5,4,3,2,1,0:T(8,128)(2,1)} %get-tuple-element.6.feat_hbm, f32[16,2304]{1,0:T(8,128)} %get-tuple-element.7.sums_ref, f32[18,128]{1,0:T(8,128)} %bitcast.5), custom_call_target="tpu_custom_call" | custom-call | tf_op jit(solution)/shard_map/finish/pallas_call | solution.py:608

commit v5 on v4

--- a/solution.py
+++ b/solution.py
@@ -92,7 +92,7 @@
         for k in ks:
             self.copy(part, k, True).wait_recv()
 
-    def steps(self, p, arrived):
+    def steps(self, p):
         plane = {d: 6 + 3 * i for i, d in enumerate(OUTWARD)}
 
         def go_on(d):
@@ -112,20 +112,11 @@
         def far_planes():
             self.wait(p, 5)
             self.start(p, plane[2], plane[2] + 1)
-            arrived(p, 0)
-
-        def far_near():
-            go_on(-1)
-            go_on(1)
-            go_on(2)
-
-        def last():
-            arrived(p, -1)
-            arrived(p, 1)
+
+        def far_arrivals():
             self.wait(p, *(plane[d] + 2 for d in OUTWARD))
-            arrived(p, 2)
-
-        return lines, near_planes, far_planes, far_near, last
+
+        return lines, near_planes, far_planes, [functools.partial(go_on, d) for d in (-1, 1, 2)], far_arrivals
 
     def drain(self):
         for copy in self.started:
@@ -191,14 +182,14 @@
             raw(p, 1)
             produce(p, -1)
             raw(p, -1)
-        for p in parts:
-            produce(p, 0)
         for d in INWARD:
             way = FAR_WAY[d]
             for p in parts:
                 idx, value = self.add(p, (None, d, way), (plane[d],))
                 self.total[idx] = value.astype(BF16)
                 self.start(p, plane[d] + (1 if way == 1 else 2))
+        for p in parts:
+            produce(p, 0)
         for i, d in enumerate(INWARD):
             for p in parts:
                 idx, value = self.add(p, (None, d, 0), (plane[d] + 1, plane[d] + 2))
@@ -223,23 +214,24 @@
     (1, 3), (3, 1), (3, 3), (0, 1), (0, 3), (1, 0), (3, 0), (0, 0),
 )
 HALF = len(MOVES) // 2
-TILE = 256
-
-
-def tiles(size, body):
+TILE = 768
+HIDDEN_TILE = 512
+
+
+def tiles(size, body, tile=TILE):
     def step(i, carry):
-        body(pl.ds(pl.multiple_of(i * TILE, TILE), TILE))
+        body(pl.ds(pl.multiple_of(i * tile, tile), tile))
         return carry
 
-    lax.fori_loop(0, size // TILE, step, 0)
+    lax.fori_loop(0, size // tile, step, 0)
 
 
 def layer_kernel(
-    tokens_ref, ids_ref, weights_ref, gate_hbm, up_hbm, down_hbm, sgate_hbm, sup_hbm, sdown_hbm,
+    tokens_hbm, ids_ref, weights_ref, gate_hbm, up_hbm, down_hbm, sgate_hbm, sup_hbm, sdown_hbm,
     enc_hbm, bias_ref, dec_hbm, feat_hbm, rec_ref,
     gate, up, down, sgate, sup, sdown, meta, metas, partial, combine, outgoing, received, hidden, served, returned,
     parts_out, parts_in, gathered, total, planes, lines, blocks, scores, feats, enc, dec, bias,
-    local_sem, meta_send, meta_recv, go_send, go_recv, back_send, back_recv, part_send, part_recv,
+    tokens_ref, local_sem, meta_send, meta_recv, go_send, go_recv, back_send, back_recv, part_send, part_recv,
     ag_send, ag_recv, rs_send, rs_recv, cross_send, cross_recv,
 ):
     torus = Torus()
@@ -262,14 +254,15 @@
             )
         )
     ]
-    for copy in weight_copies:
-        copy.start()
+    tokens_copy = pltpu.make_async_copy(tokens_hbm, tokens_ref, local_sem.at[10])
     feat_sem = local_sem.at[9]
 
     meta[...] = jnp.zeros_like(meta)
     meta[:TOP, :own_rows] = ids_ref[...].astype(F32)
     meta[TOP:, :own_rows] = weights_ref[...]
     metas[f] = meta[...]
+    for copy in [tokens_copy] + weight_copies:
+        copy.start()
 
     def plane(move, sign=1):
         dy, dx = move
@@ -294,6 +287,7 @@
 
     for copy in weight_copies[:3]:
         copy.wait()
+    tokens_copy.wait()
     tokens = tokens_ref[...]
     shared_gate = jnp.dot(tokens, sgate[...], preferred_element_type=F32)
     shared_up = jnp.dot(tokens, sup[...], preferred_element_type=F32)
@@ -379,14 +373,7 @@
             up_proj = jnp.dot(x, up[:, cols], preferred_element_type=F32)
             hidden[half, :, cols] = (jax.nn.silu(gate_proj) * up_proj).astype(BF16)
 
-        tiles(hidden.shape[2], inner)
-
-    def part_tiles(p, body):
-        def step(i, carry):
-            body(pl.ds(pl.multiple_of(p * width + i * TILE, TILE), TILE))
-            return carry
-
-        lax.fori_loop(0, width // TILE, step, 0)
+        tiles(hidden.shape[2], inner, HIDDEN_TILE)
 
     def back_copy(p, i, sign):
         cols = pl.ds(p * width, width)
@@ -402,7 +389,7 @@
         returned[n_e - 1, :, cols] = value[n_e - 1]
 
     for p in range(PARTS):
-        part_tiles(p, outer)
+        outer(pl.ds(p * width, width))
         for i in range(n_e - 1):
             send(back_copy(p, i, -1))
 
@@ -430,8 +417,8 @@
     def give(p):
         for i in range(n_e - 1):
             back_copy(p, i, 1).wait_recv()
-        part_tiles(p, share)
         cols = pl.ds(p * width, width)
+        share(cols)
         for i in range(1, n_f):
             there = column(i)
             copy = remote(
@@ -453,24 +440,31 @@
     def encode(p, delta):
         idx = torus.index(p, (None, None, delta))
 
-        def step(i, carry):
-            which = i // (features // TILE)
-            cols = pl.ds(pl.multiple_of(lax.rem(i, features // TILE) * TILE, TILE), TILE)
-            block = gathered[(p, *idx)].reshape(SIDE * SIDE * own_rows, width)
-            value = jnp.dot(block, enc[which, p * width : (p + 1) * width, cols], preferred_element_type=F32)
-            at = (which, *idx, ALL, cols)
-            scores[at] = scores[at] + value.reshape(SIDE, SIDE, own_rows, TILE)
-            return carry
-
-        lax.fori_loop(0, 2 * features // TILE, step, 0)
-
-    steps = [
-        [functools.partial(give, p), functools.partial(take, p), *gather.steps(p, encode)] for p in range(PARTS)
+        block = gathered[(p, *idx)].reshape(SIDE * SIDE * own_rows, width)
+        for which in range(2):
+            value = jnp.dot(block, enc[which, p * width : (p + 1) * width, :], preferred_element_type=F32)
+            at = (which, *idx)
+            scores[at] = scores[at] + value.reshape(SIDE, SIDE, own_rows, features)
+
+    steps = [gather.steps(p) for p in range(PARTS)]
+    early = [
+        [functools.partial(give, p), functools.partial(take, p), *steps[p][:3]] for p in range(PARTS)
     ]
-    for turn in range(len(steps[0]) + PARTS - 1):
+    for turn in range(len(early[0]) + PARTS - 1):
         for p in reversed(range(PARTS)):
-            if 0 <= turn - p < len(steps[p]):
-                steps[p][turn - p]()
+            if 0 <= turn - p < len(early[p]):
+                early[p][turn - p]()
+    for p in range(PARTS):
+        encode(p, 0)
+    for i in range(3):
+        for p in range(PARTS):
+            steps[p][3][i]()
+    for p in range(PARTS):
+        encode(p, -1)
+        encode(p, 1)
+    for p in range(PARTS):
+        steps[p][4]()
+        encode(p, 2)
 
     def rectify(y, carry):
         for which in range(2):
@@ -492,18 +486,13 @@
 
     def produce(p, delta):
         idx = torus.index(p, (None, None, delta))
-        left = [feats[(which, *idx)].reshape(SIDE * SIDE * own_rows, features) for which in range(2)]
-
-        def step(i, carry):
-            cols = pl.ds(pl.multiple_of(i * TILE, TILE), TILE)
-            here = pl.ds(pl.multiple_of(p * width + i * TILE, TILE), TILE)
-            value = jnp.dot(left[0], dec[0, :, here], preferred_element_type=F32) + jnp.dot(
-                left[1], dec[1, :, here], preferred_element_type=F32
+        value = 0.0
+        for which in range(2):
+            block = feats[(which, *idx)].reshape(SIDE * SIDE * own_rows, features)
+            value = value + jnp.dot(
+                block, dec[which, :, p * width : (p + 1) * width], preferred_element_type=F32
             )
-            total[(p, *idx, ALL, cols)] = value.astype(BF16).reshape(SIDE, SIDE, own_rows, TILE)
-            return carry
-
-        lax.fori_loop(0, width // TILE, step, 0)
+        total[(p, *idx)] = value.astype(BF16).reshape(SIDE, SIDE, own_rows, width)
 
     def finish(p, value):
         rec_ref[:, p * width : (p + 1) * width] = value
@@ -541,7 +530,7 @@
             jax.ShapeDtypeStruct((*cube, 2, own_rows, features), BF16),
             jax.ShapeDtypeStruct((own_rows, model), F32),
         ),
-        in_specs=[vmem] * 3 + [hbm] * 7 + [vmem, hbm],
+        in_specs=[hbm] + [vmem] * 2 + [hbm] * 7 + [vmem, hbm],
         out_specs=(hbm, vmem),
         scratch_shapes=[pltpu.VMEM(w.shape[1:], BF16) for w in routed]
         + [pltpu.VMEM(w.shape, BF16) for w in shared]
@@ -567,7 +556,8 @@
             pltpu.VMEM((2, model, features), BF16),
             pltpu.VMEM((2, features, model), BF16),
             pltpu.VMEM((2, 1, features), F32),
-            dma((10,)),
+            pltpu.VMEM(tokens.shape, BF16),
+            dma((11,)),
             dma((n_f - 1,)),
             dma((n_f - 1,)),
             dma((n_e - 1,)),
@@ -586,25 +576,33 @@
     )(tokens, ids, weights, *routed, *shared, encoder, encoder_bias, decoder)
 
 
-def finish_kernel(feat_hbm, sums_ref, bias_ref, out_hbm, rec_ref, held, in_sem, out_sem):
-    reads = [pltpu.make_async_copy(feat_hbm.at[y], held.at[y], in_sem.at[y]) for y in range(SIDE)]
-    writes = [pltpu.make_async_copy(held.at[y], out_hbm.at[y], out_sem.at[y]) for y in range(SIDE)]
+def finish_kernel(feat_hbm, sums_hbm, bias_hbm, out_hbm, rec_hbm, held, sums, bias, in_sem, out_sem):
+    reads = [
+        pltpu.make_async_copy(sums_hbm, sums, in_sem.at[SIDE]),
+        pltpu.make_async_copy(bias_hbm, bias, in_sem.at[SIDE + 1]),
+    ] + [pltpu.make_async_copy(feat_hbm.at[y], held.at[y], in_sem.at[y]) for y in range(SIDE)]
+    writes = [pltpu.make_async_copy(sums, rec_hbm, out_sem.at[SIDE])] + [
+        pltpu.make_async_copy(held.at[y], out_hbm.at[y], out_sem.at[y]) for y in range(SIDE)
+    ]
     for copy in reads:
         copy.start()
-    lanes = bias_ref.shape[1]
-    for i in range(bias_ref.shape[0]):
+    reads[0].wait()
+    reads[1].wait()
+    lanes = bias.shape[1]
+    for i in range(bias.shape[0]):
         cols = slice(i * lanes, (i + 1) * lanes)
-        rec_ref[:, cols] = sums_ref[:, cols] + bias_ref[i : i + 1, :]
+        sums[:, cols] = sums[:, cols] + bias[i : i + 1, :]
     for y in range(SIDE):
-        reads[y].wait()
-        writes[y].start()
+        reads[2 + y].wait()
+        writes[1 + y].start()
+    writes[0].start()
     for copy in writes:
         copy.wait()
 
 
 def finish(features, sums, bias):
-    vmem = pl.BlockSpec(memory_space=pltpu.VMEM)
     hbm = pl.BlockSpec(memory_space=pl.ANY)
+    bias = bias.reshape(-1, 128)
     return pl.pallas_call(
         finish_kernel,
         name="finish",
@@ -612,15 +610,17 @@
             jax.ShapeDtypeStruct(features.shape, features.dtype),
             jax.ShapeDtypeStruct(sums.shape, sums.dtype),
         ),
-        in_specs=[hbm, vmem, vmem],
-        out_specs=(hbm, vmem),
+        in_specs=[hbm] * 3,
+        out_specs=(hbm, hbm),
         scratch_shapes=[
             pltpu.VMEM(features.shape, features.dtype),
-            pltpu.SemaphoreType.DMA((SIDE,)),
-            pltpu.SemaphoreType.DMA((SIDE,)),
+            pltpu.VMEM(sums.shape, sums.dtype),
+            pltpu.VMEM(bias.shape, bias.dtype),
+            pltpu.SemaphoreType.DMA((SIDE + 2,)),
+            pltpu.SemaphoreType.DMA((SIDE + 1,)),
         ],
         compiler_params=pltpu.CompilerParams(vmem_limit_bytes=60 * 1024 * 1024),
-    )(features, sums, bias.reshape(-1, 128))
+    )(features, sums, bias)
 
 
 def shards(

time: 121 us -> 111 us (0.917)
  Pallas kernels: 121 us -> 110 us
    pallas_call x1, Pallas kernels: 117 us -> 107 us  [layer(): pl.pallas_call(layer_kernel, name='layer', out_shape=(jax.ShapeDtypeStruc...]
    pallas_call x1, Pallas kernels: 3.99 us -> 2.59 us  [finish(): pl.pallas_call(finish_kernel, name='finish', out_shape=(jax.ShapeDtypeStr...]
where the time goes in v5:
time: 111 us; the launch traced here: 110 us
  Pallas kernels  110 us (99%)
    pallas_call x1, Pallas kernels, layer(): pl.pallas_call(layer_kernel, name='layer', out_shape=(jax.ShapeDtypeStruc...  107 us
    pallas_call x1, Pallas kernels, finish(): pl.pallas_call(finish_kernel, name='finish', out_shape=(jax.ShapeDtypeStr...  2.59 us

profile of v5, /device:TPU:0, one launch (start us, length us, event | category | flops | bytes accessed | tf_op | source)
XLA Modules:
  0.0 110.5 jit_solution(15088200018901344730)
XLA Ops:
  0.6 107.1 %layer.1 = (bf16[4,4,4,2,16,512]{5,4,3,2,1,0:T(8,128)(2,1)}, f32[16,2304]{1,0:T(8,128)}) custom-call(bf16[128,2304]{1,0:T(8,128)(2,1)} %tokens_hbm.1, s32[8,16]{1,0:T(8,128)} %bitcast.6, f32[8,16]{1,0:T(8,128)} %bitcast.7, bf16[1,2304,1024]{2,1,0:T(8,128)(2,1)} %gate_hbm.1, bf16[1,2304,1024]{2,1,0:T(8,128)(2,1)} %up_hbm.1, bf16[1,1024,2304]{2,1,0:T(8,128)(2,1)} %down_hbm.1, ...), custom_call_target="tpu_custom_call" | custom-call | tf_op jit(solution)/shard_map/layer/pallas_call | solution.py:526
  107.7 2.6 %finish.1 = (bf16[4,4,4,2,16,512]{5,4,3,2,1,0:T(8,128)(2,1)}, f32[16,2304]{1,0:T(8,128)}) custom-call(bf16[4,4,4,2,16,512]{5,4,3,2,1,0:T(8,128)(2,1)} %get-tuple-element.6.feat_hbm, f32[16,2304]{1,0:T(8,128)} %get-tuple-element.7.sums_hbm, f32[18,128]{1,0:T(8,128)} %bitcast.5), custom_call_target="tpu_custom_call" | custom-call | tf_op jit(solution)/shard_map/finish/pallas_call | solution.py:606

commit v6 on v5

--- a/solution.py
+++ b/solution.py
@@ -45,12 +45,6 @@
             idx[axis] = ALL if delta is None else self.at(axis, delta)
         return tuple(idx)
 
-    def meet(self, peers):
-        barrier = pltpu.get_barrier_semaphore()
-        for there in peers:
-            pl.semaphore_signal(barrier, inc=1, device_id=there, device_id_type=MESH)
-        pl.semaphore_wait(barrier, len(peers))
-
 
 def remote(src, dst, send, recv, where):
     return pltpu.make_async_remote_copy(
@@ -59,8 +53,8 @@
 
 
 class Gather:
-    def __init__(self, torus, buf, send, recv):
-        self.torus, self.buf, self.send, self.recv = torus, buf, send, recv
+    def __init__(self, torus, bufs, send, recv):
+        self.torus, self.bufs, self.send, self.recv = torus, bufs, send, recv
         self.specs = [(0, d, (0, 0, 0), (-d, 0, 0)) for d in OTHERS]
         self.specs += [(1, d, (None, 0, 0), (None, -d, 0)) for d in OTHERS]
         for d in OUTWARD:
@@ -73,7 +67,7 @@
         self.started = []
 
     def cells(self, part, offsets):
-        return self.buf.at[(part, *self.torus.index(part, offsets))]
+        return self.bufs[part].at[self.torus.index(part, offsets)]
 
     def copy(self, part, k, landing):
         slot, delta, source, target = self.specs[k]
@@ -216,6 +210,7 @@
 HALF = len(MOVES) // 2
 TILE = 768
 HIDDEN_TILE = 512
+SPLIT = (0, 896, 1664, 2304)
 
 
 def tiles(size, body, tile=TILE):
@@ -227,11 +222,11 @@
 
 
 def layer_kernel(
-    tokens_hbm, ids_ref, weights_ref, gate_hbm, up_hbm, down_hbm, sgate_hbm, sup_hbm, sdown_hbm,
-    enc_hbm, bias_ref, dec_hbm, feat_hbm, rec_ref,
+    tokens_hbm, ids_hbm, weights_hbm, gate_hbm, up_hbm, down_hbm, sgate_hbm, sup_hbm, sdown_hbm,
+    enc_hbm, bias_hbm, dec_hbm, feat_hbm, rec_ref,
     gate, up, down, sgate, sup, sdown, meta, metas, partial, combine, outgoing, received, hidden, served, returned,
-    parts_out, parts_in, gathered, total, planes, lines, blocks, scores, feats, enc, dec, bias,
-    tokens_ref, local_sem, meta_send, meta_recv, go_send, go_recv, back_send, back_recv, part_send, part_recv,
+    parts_out, parts_in, gathered0, gathered1, gathered2, total, planes, lines, blocks, scores, feats, enc, dec, bias,
+    tokens_ref, ids_ref, weights_ref, local_sem, meta_send, meta_recv, go_send, go_recv, back_send, back_recv, part_send, part_recv,
     ag_send, ag_recv, rs_send, rs_recv, cross_send, cross_recv,
 ):
     torus = Torus()
@@ -241,7 +236,8 @@
     rows = n_f * own_rows
     slots = n_e * own_rows
     chunk = HALF * own_rows
-    width = gathered.shape[-1]
+    width = total.shape[-1]
+    gathered = (gathered0, gathered1, gathered2)
     features = enc.shape[2]
 
     weight_copies = [
@@ -250,32 +246,39 @@
             (
                 (sgate_hbm, sgate), (sup_hbm, sup), (sdown_hbm, sdown),
                 (gate_hbm.at[0], gate), (up_hbm.at[0], up), (down_hbm.at[0], down),
-                (enc_hbm, enc.at[core]), (bias_ref, bias.at[core]), (dec_hbm, dec.at[core]),
+                (enc_hbm, enc.at[core]), (bias_hbm, bias.at[core]), (dec_hbm, dec.at[core]),
             )
         )
     ]
     tokens_copy = pltpu.make_async_copy(tokens_hbm, tokens_ref, local_sem.at[10])
     feat_sem = local_sem.at[9]
 
+    choice_copies = [
+        pltpu.make_async_copy(ids_hbm, ids_ref, local_sem.at[11]),
+        pltpu.make_async_copy(weights_hbm, weights_ref, local_sem.at[12]),
+    ]
+    for copy in choice_copies + [tokens_copy] + weight_copies:
+        copy.start()
+
+    def plane(move, sign=1):
+        dy, dx = move
+        y = lax.rem(torus.pos[0] + SIDE + sign * dy, SIDE)
+        return y * SIDE + lax.rem(torus.pos[1] + SIDE + sign * dx, SIDE)
+
+    def column(i):
+        return lax.rem(f + i, n_f)
+
+    barrier = pltpu.get_barrier_semaphore()
+    peers = [(plane(m), f) for m in MOVES[:-1]] + [(e, column(i)) for i in range(1, n_f)]
+    for there in peers:
+        pl.semaphore_signal(barrier, inc=1, device_id=there, device_id_type=MESH)
+    for copy in choice_copies:
+        copy.wait()
     meta[...] = jnp.zeros_like(meta)
     meta[:TOP, :own_rows] = ids_ref[...].astype(F32)
     meta[TOP:, :own_rows] = weights_ref[...]
     metas[f] = meta[...]
-    for copy in [tokens_copy] + weight_copies:
-        copy.start()
-
-    def plane(move, sign=1):
-        dy, dx = move
-        y = lax.rem(torus.pos[0] + SIDE + sign * dy, SIDE)
-        return y * SIDE + lax.rem(torus.pos[1] + SIDE + sign * dx, SIDE)
-
-    def column(i):
-        return lax.rem(f + i, n_f)
-
-    torus.meet(
-        [(plane(m), f) for m in MOVES[:-1]]
-        + [(e, column(i)) for i in range(1, n_f)]
-    )
+    pl.semaphore_wait(barrier, len(peers))
     sent = []
 
     def send(copy):
@@ -375,8 +378,11 @@
 
         tiles(hidden.shape[2], inner, HIDDEN_TILE)
 
+    def part_cols(p):
+        return pl.ds(SPLIT[p], SPLIT[p + 1] - SPLIT[p])
+
     def back_copy(p, i, sign):
-        cols = pl.ds(p * width, width)
+        cols = part_cols(p)
         return remote(
             served.at[i, :, cols], returned.at[i, :, cols],
             back_send.at[p, i], back_recv.at[p, i], (plane(MOVES[i], sign), f),
@@ -384,12 +390,12 @@
 
     def outer(cols):
         value = jnp.dot(hidden[...].reshape(slots, hidden.shape[2]), down[:, cols], preferred_element_type=F32)
-        value = value.astype(BF16).reshape(n_e, own_rows, TILE)
+        value = value.astype(BF16).reshape(n_e, own_rows, -1)
         served[:, :, cols] = value
         returned[n_e - 1, :, cols] = value[n_e - 1]
 
     for p in range(PARTS):
-        outer(pl.ds(p * width, width))
+        outer(part_cols(p))
         for i in range(n_e - 1):
             send(back_copy(p, i, -1))
 
@@ -406,18 +412,18 @@
     incoming = {}
 
     def share(cols):
-        back = returned[:, :, cols].reshape(slots, TILE)
-        value = partial[:, :, cols].reshape(rows, TILE)
+        back = returned[:, :, cols].reshape(slots, -1)
+        value = partial[:, :, cols].reshape(rows, -1)
         for i in range(2):
             value = value + jnp.dot(combine[i], back, preferred_element_type=F32)
-        value = value.reshape(n_f, own_rows, TILE)
+        value = value.reshape(n_f, own_rows, -1)
         partial[:, :, cols] = value
         parts_out[:, :, cols] = value.astype(BF16)
 
     def give(p):
         for i in range(n_e - 1):
             back_copy(p, i, 1).wait_recv()
-        cols = pl.ds(p * width, width)
+        cols = part_cols(p)
         share(cols)
         for i in range(1, n_f):
             there = column(i)
@@ -429,20 +435,20 @@
             incoming[p, i] = copy
 
     def take(p):
-        cols = pl.ds(p * width, width)
+        cols = part_cols(p)
         value = partial[f, :, cols]
         for i in range(1, n_f):
             incoming[p, i].wait_recv()
             value = value + parts_in[i - 1, :, cols].astype(F32)
-        gathered[(p, *torus.pos)] = value.astype(BF16)
+        gathered[p][torus.pos] = value.astype(BF16)
         gather.start(p, 0, 1, 2)
 
     def encode(p, delta):
         idx = torus.index(p, (None, None, delta))
 
-        block = gathered[(p, *idx)].reshape(SIDE * SIDE * own_rows, width)
+        block = gathered[p][idx].reshape(SIDE * SIDE * own_rows, -1)
         for which in range(2):
-            value = jnp.dot(block, enc[which, p * width : (p + 1) * width, :], preferred_element_type=F32)
+            value = jnp.dot(block, enc[which, SPLIT[p] : SPLIT[p + 1], :], preferred_element_type=F32)
             at = (which, *idx)
             scores[at] = scores[at] + value.reshape(SIDE, SIDE, own_rows, features)
 
@@ -466,12 +472,11 @@
         steps[p][4]()
         encode(p, 2)
 
-    def rectify(y, carry):
+    def rectify(delta):
+        idx = torus.index(0, (None, None, delta))
         for which in range(2):
-            feats[which, y] = jnp.maximum(scores[which, y], 0.0).astype(BF16)
-        return carry
-
-    lax.fori_loop(0, SIDE, rectify, 0)
+            feats[(which, *idx)] = jnp.maximum(scores[(which, *idx)], 0.0).astype(BF16)
+
     own_out = pltpu.make_async_copy(feats.at[core], feat_hbm.at[:, :, :, core], feat_sem)
     cross_out = remote(
         feats.at[other], feat_hbm.at[:, :, :, core], cross_send.at[3], cross_recv.at[3], partner
@@ -479,12 +484,17 @@
     cross_in = remote(
         feats.at[other], feat_hbm.at[:, :, :, other], cross_send.at[3], cross_recv.at[3], partner
     )
-    own_out.start()
-    cross_out.start()
 
     scatter = Scatter(torus, total, planes, lines, blocks, rs_send, rs_recv)
 
     def produce(p, delta):
+        if (p, delta) == (0, 2):
+            rectify(2)
+        if (p, delta) == (1, 2):
+            for d in (0, 1, -1):
+                rectify(d)
+            own_out.start()
+            cross_out.start()
         idx = torus.index(p, (None, None, delta))
         value = 0.0
         for which in range(2):
@@ -530,7 +540,7 @@
             jax.ShapeDtypeStruct((*cube, 2, own_rows, features), BF16),
             jax.ShapeDtypeStruct((own_rows, model), F32),
         ),
-        in_specs=[hbm] + [vmem] * 2 + [hbm] * 7 + [vmem, hbm],
+        in_specs=[hbm] * 12,
         out_specs=(hbm, vmem),
         scratch_shapes=[pltpu.VMEM(w.shape[1:], BF16) for w in routed]
         + [pltpu.VMEM(w.shape, BF16) for w in shared]
@@ -546,7 +556,7 @@
             plane_rows,
             pltpu.VMEM((n_f, own_rows, model), BF16),
             pltpu.VMEM((n_f - 1, own_rows, model), BF16),
-            pltpu.VMEM((PARTS, *cube, own_rows, width), BF16),
+            *(pltpu.VMEM((*cube, own_rows, SPLIT[p + 1] - SPLIT[p]), BF16) for p in range(PARTS)),
             pltpu.VMEM((PARTS, *cube, own_rows, width), BF16),
             pltpu.VMEM((PARTS, 3, SIDE, SIDE, own_rows, width), BF16),
             pltpu.VMEM((PARTS, 3, SIDE, own_rows, width), BF16),
@@ -557,7 +567,9 @@
             pltpu.VMEM((2, features, model), BF16),
             pltpu.VMEM((2, 1, features), F32),
             pltpu.VMEM(tokens.shape, BF16),
-            dma((11,)),
+            pltpu.VMEM(ids.shape, ids.dtype),
+            pltpu.VMEM(weights.shape, weights.dtype),
+            dma((13,)),
             dma((n_f - 1,)),
             dma((n_f - 1,)),
             dma((n_e - 1,)),

time: 111 us -> 111 us (level)
  no operation moved by 1% of the time
where the time goes in v6:
time: 111 us
  Pallas kernels  110 us (99%)
    pallas_call x1, Pallas kernels, layer(): pl.pallas_call(layer_kernel, name='layer', out_shape=(jax.ShapeDtypeStruc...  108 us
    pallas_call x1, Pallas kernels, finish(): pl.pallas_call(finish_kernel, name='finish', out_shape=(jax.ShapeDtypeStr...  2.59 us

profile of v6, /device:TPU:0, one launch (start us, length us, event | category | flops | bytes accessed | tf_op | source)
XLA Modules:
  0.0 111.1 jit_solution(10993417533826555017)
XLA Ops:
  0.6 107.7 %layer.1 = (bf16[4,4,4,2,16,512]{5,4,3,2,1,0:T(8,128)(2,1)}, f32[16,2304]{1,0:T(8,128)}) custom-call(bf16[128,2304]{1,0:T(8,128)(2,1)} %tokens_hbm.1, s32[8,16]{1,0:T(8,128)} %bitcast.6, f32[8,16]{1,0:T(8,128)} %bitcast.7, bf16[1,2304,1024]{2,1,0:T(8,128)(2,1)} %gate_hbm.1, bf16[1,2304,1024]{2,1,0:T(8,128)(2,1)} %up_hbm.1, bf16[1,1024,2304]{2,1,0:T(8,128)(2,1)} %down_hbm.1, ...), custom_call_target="tpu_custom_call" | custom-call | tf_op jit(solution)/shard_map/layer/pallas_call | solution.py:536
  108.3 2.6 %finish.1 = (bf16[4,4,4,2,16,512]{5,4,3,2,1,0:T(8,128)(2,1)}, f32[16,2304]{1,0:T(8,128)}) custom-call(bf16[4,4,4,2,16,512]{5,4,3,2,1,0:T(8,128)(2,1)} %get-tuple-element.6.feat_hbm, f32[16,2304]{1,0:T(8,128)} %get-tuple-element.7.sums_hbm, f32[18,128]{1,0:T(8,128)} %bitcast.5), custom_call_target="tpu_custom_call" | custom-call | tf_op jit(solution)/shard_map/finish/pallas_call | solution.py:618

commit v7 on v6

--- a/solution.py
+++ b/solution.py
@@ -210,7 +210,7 @@
 HALF = len(MOVES) // 2
 TILE = 768
 HIDDEN_TILE = 512
-SPLIT = (0, 896, 1664, 2304)
+SPLIT = (0, 1024, 1792, 2304)
 
 
 def tiles(size, body, tile=TILE):

time: 111 us -> 113 us (1.018)
  Pallas kernels: 110 us -> 112 us
    pallas_call x1, Pallas kernels: 108 us -> 109 us  [layer(): pl.pallas_call(layer_kernel, name='layer', out_shape=(jax.ShapeDtypeStruc...]
where the time goes in v7:
time: 113 us
  Pallas kernels  112 us (99%)
    pallas_call x1, Pallas kernels, layer(): pl.pallas_call(layer_kernel, name='layer', out_shape=(jax.ShapeDtypeStruc...  109 us
    pallas_call x1, Pallas kernels, finish(): pl.pallas_call(finish_kernel, name='finish', out_shape=(jax.ShapeDtypeStr...  2.59 us

profile of v7, /device:TPU:0, one launch (start us, length us, event | category | flops | bytes accessed | tf_op | source)
XLA Modules:
  0.0 112.8 jit_solution(1889458953133018234)
XLA Ops:
  0.6 109.5 %layer.1 = (bf16[4,4,4,2,16,512]{5,4,3,2,1,0:T(8,128)(2,1)}, f32[16,2304]{1,0:T(8,128)}) custom-call(bf16[128,2304]{1,0:T(8,128)(2,1)} %tokens_hbm.1, s32[8,16]{1,0:T(8,128)} %bitcast.6, f32[8,16]{1,0:T(8,128)} %bitcast.7, bf16[1,2304,1024]{2,1,0:T(8,128)(2,1)} %gate_hbm.1, bf16[1,2304,1024]{2,1,0:T(8,128)(2,1)} %up_hbm.1, bf16[1,1024,2304]{2,1,0:T(8,128)(2,1)} %down_hbm.1, ...), custom_call_target="tpu_custom_call" | custom-call | tf_op jit(solution)/shard_map/layer/pallas_call | solution.py:536
  110.1 2.6 %finish.1 = (bf16[4,4,4,2,16,512]{5,4,3,2,1,0:T(8,128)(2,1)}, f32[16,2304]{1,0:T(8,128)}) custom-call(bf16[4,4,4,2,16,512]{5,4,3,2,1,0:T(8,128)(2,1)} %get-tuple-element.6.feat_hbm, f32[16,2304]{1,0:T(8,128)} %get-tuple-element.7.sums_hbm, f32[18,128]{1,0:T(8,128)} %bitcast.5), custom_call_target="tpu_custom_call" | custom-call | tf_op jit(solution)/shard_map/finish/pallas_call | solution.py:618
